TPU v7x, 32 devices: a whole 2x2x4 slice. The times are simulated.
32 devices in a mesh: gy: 4 (over y, core), gx: 8 (over z, x).
Axes of the slice: x: 2, y: 2, z: 4, core: 2. Of those that a mesh axis runs over, the one named last changes fastest.
Arguments:
- features: bfloat16 [256, 512, 128], P(('gy', 'gx')), may hold values from -6 to 6
- links: int32 [256, 3], P(('gy', 'gx')), may hold values 0 or 1
- block_slot: int32 [256], P(('gy', 'gx')), may hold values from 0 to 15, as said below
- block_level: int32 [256], P(('gy', 'gx')), may hold values from 0 to 3
- slot_column: int32 [32, 16], P(('gy', 'gx')), may hold values from 0 to 31
- conv_first: bfloat16 [7, 128, 128], replicated, may hold values from -0.1875 to 0.1875
- conv_second: bfloat16 [7, 128, 128], replicated, may hold values from -0.1875 to 0.1875
- height_w: bfloat16 [4, 1024, 256], replicated, may hold values from -0.1875 to 0.1875
- plane_first: bfloat16 [3, 3, 256, 256], replicated, may hold values from -0.125 to 0.125
- plane_second: bfloat16 [3, 3, 256, 256], replicated, may hold values from -0.125 to 0.125
Outputs:
- bev_out: bfloat16 [256, 256, 256], P('gy', 'gx')
Inputs may be any that keep to these rules, and one draw needn't show every extreme that they name: No two blocks of one device have both the same block_slot and the same block_level. At most 4 blocks of one device have the same block_slot // 2, and every device has exactly 4 such blocks for some value.
All inputs are finite; a program needn't handle non-finite values. No bound on the sum of `links` on one device may be relied on, other than what follows from the above.
Results may differ from a plain program's by a relative error of at most 0.0065.
Values may be sent and summed in bfloat16 or wider, within the bound.
No kernel may reach another device: no remote copies, remote signals or barrier semaphores. Data moves between devices by JAX's collectives and lax.ppermute only.
A program may use at most 64 MiB of HBM per device.

v0:
```python
import jax
import jax.numpy as jnp
from jax import lax
from jax.experimental import pallas as pl
from jax.experimental.pallas import tpu as pltpu
from jax.sharding import PartitionSpec as P


EDGE = 8
FACE = EDGE * EDGE
CELLS = EDGE * FACE
TILE_BR = 8
TILE_BC = 4
ROWS = TILE_BR * EDGE
COLS = TILE_BC * EDGE
HALO = 2
ID_ROWS = 8
LANES = 128
F32 = jnp.float32
BF16 = jnp.bfloat16

VMEM = pl.BlockSpec(memory_space=pltpu.VMEM)
SMEM = pl.BlockSpec(memory_space=pltpu.SMEM)
ANY = pl.BlockSpec(memory_space=pl.ANY)


def swap(first, second, axis):
    count = lax.axis_size(axis)
    near = [(i, i ^ 1) for i in range(count) if i ^ 1 < count]
    far = [(i, i + 1 if i % 2 else i - 1) for i in range(1, count)]
    far = [(i, k) for i, k in far if k < count]
    first = lax.ppermute(first, axis, near)
    second = lax.ppermute(second, axis, far)
    return first, second


def trade_order(count):
    assert count & (count - 1) == 0
    far, near = range(count // 2, count), range(1, count // 2)
    return [k for half in (far, near) for odd in (1, 0) for k in half if k % 2 == odd]


def route(odd, up, down, first, second):
    @pl.when(odd == 0)
    def _():
        first[...] = up[...]
        second[...] = down[...]

    @pl.when(odd != 0)
    def _():
        first[...] = down[...]
        second[...] = up[...]


def mm(a, b):
    return jnp.dot(a, b, preferred_element_type=F32)


def link_of(links, block, axis):
    return links[axis, block].astype(F32)


def pack_faces(src, links, up, down):
    count = src.shape[0] // CELLS
    faces = count * FACE
    upper_b, lower_b = [], []
    for j in range(count):
        keep = link_of(links, j, 1)
        for a in range(EDGE):
            base = j * CELLS + a * FACE
            upper_b.append(src[base + FACE - EDGE : base + FACE, :] * keep)
            lower_b.append(src[base : base + EDGE, :])
    up[0:faces, :] = jnp.concatenate(upper_b, 0).astype(BF16)
    down[0:faces, :] = jnp.concatenate(lower_b, 0).astype(BF16)
    upper_c = []
    for j in range(count):
        upper_c.append(
            src[pl.ds(j * CELLS + EDGE - 1, FACE, stride=EDGE), :] * link_of(links, j, 2)
        )
    up[faces : 2 * faces, :] = jnp.concatenate(upper_c, 0).astype(BF16)
    down[faces : 2 * faces, :] = src[pl.ds(0, faces, stride=EDGE), :].astype(BF16)
    last = count * CELLS
    up[2 * faces :, :] = (src[last - FACE : last, :] * link_of(links, count - 1, 0)).astype(BF16)
    down[2 * faces :, :] = src[0:FACE, :].astype(BF16)


def pack_kernel(links, x, first, second, wide, up, down):
    wide[...] = x[...].astype(F32)
    pack_faces(wide, links, up, down)
    route(links[3, 4], up, down, first, second)


def interior(src, links, weights, out, residual):
    count = src.shape[0] // CELLS
    c_at = lax.broadcasted_iota(jnp.int32, (FACE, EDGE, 128), 1)

    def one(j, carry):
        base = pl.multiple_of(j * CELLS, CELLS)
        rows = src[pl.ds(base, CELLS), :]
        after = jnp.minimum(j + 1, count - 1)
        before = jnp.maximum(j - 1, 0)
        keep_after = jnp.where(j + 1 < count, links[0, j], 0).astype(F32)
        keep_before = jnp.where(j > 0, links[0, before], 0).astype(F32)
        over = src[pl.ds(pl.multiple_of(after * CELLS, CELLS), FACE), :]
        under = src[pl.ds(pl.multiple_of(before * CELLS + CELLS - FACE, FACE), FACE), :]
        over = (over.astype(F32) * keep_after).astype(BF16)
        under = (under.astype(F32) * keep_before).astype(BF16)
        wide = rows.astype(F32)
        planes = wide.reshape(EDGE, EDGE, EDGE, 128)
        none = jnp.zeros((EDGE, 1, EDGE, 128), F32)
        lines = wide.reshape(FACE, EDGE, 128)
        taps = [
            rows,
            jnp.concatenate([rows[FACE:], over], 0),
            jnp.concatenate([under, rows[:-FACE]], 0),
            jnp.concatenate([planes[:, 1:], none], 1).reshape(CELLS, 128).astype(BF16),
            jnp.concatenate([none, planes[:, :-1]], 1).reshape(CELLS, 128).astype(BF16),
            jnp.where(c_at == EDGE - 1, 0.0, pltpu.roll(lines, EDGE - 1, 1))
            .reshape(CELLS, 128)
            .astype(BF16),
            jnp.where(c_at == 0, 0.0, pltpu.roll(lines, 1, 1)).reshape(CELLS, 128).astype(BF16),
        ]
        total = mm(jnp.concatenate(taps, 1), weights[...])
        if residual is not None:
            total = total + residual[pl.ds(base, CELLS), :].astype(F32)
        out[pl.ds(base, CELLS), :] = total
        return carry

    lax.fori_loop(0, count, one, 0)


def first_interior_kernel(links, x, weights, out):
    interior(x, links, weights, out, None)


def second_interior_kernel(links, hidden, x, weights, out):
    interior(hidden, links, weights, out, x)


def ghost_places(count):
    faces = count * FACE
    return (0, faces, 2 * faces, 3 * faces, 4 * faces, 4 * faces + FACE)


def ghost_terms(ghosts, from_below, from_above, links, weights):
    ch = ghosts.shape[1]
    count = (from_below.shape[0] // FACE - 1) // 2
    faces = count * FACE
    b_plus, b_minus, c_plus, c_minus, a_plus, a_minus = ghost_places(count)

    def tap(k):
        return weights[k * ch : (k + 1) * ch, :]

    for start, to, axis, k in ((0, b_plus, 1, 3), (faces, c_plus, 2, 5)):
        product = mm(from_above[start : start + faces, :], tap(k))
        for j in range(count):
            rows = slice(j * FACE, (j + 1) * FACE)
            ghosts[to + j * FACE : to + (j + 1) * FACE, :] = product[rows, :] * link_of(
                links, j, axis
            )
    ghosts[b_minus : b_minus + faces, :] = mm(from_below[0:faces, :], tap(4))
    ghosts[c_minus : c_minus + faces, :] = mm(from_below[faces : 2 * faces, :], tap(6))
    product = mm(from_above[2 * faces :, :], tap(1))
    ghosts[a_plus : a_plus + FACE, :] = product * link_of(links, count - 1, 0)
    ghosts[a_minus : a_minus + FACE, :] = mm(from_below[2 * faces :, :], tap(2))


def hidden_kernel(
    links,
    partial,
    first_in,
    second_in,
    weights,
    hidden,
    first,
    second,
    total,
    up,
    down,
    from_below,
    from_above,
    ghosts,
):
    count = partial.shape[0] // CELLS
    ch = partial.shape[1]
    route(links[3, 4], first_in, second_in, from_above, from_below)
    ghost_terms(ghosts, from_below, from_above, links, weights)
    b_plus, b_minus, c_plus, c_minus, a_plus, a_minus = ghost_places(count)
    c_at = lax.broadcasted_iota(jnp.int32, (EDGE, ch), 0)
    for j in range(count):
        lines = []
        for a in range(EDGE):
            for b in range(EDGE):
                at = j * CELLS + a * FACE + b * EDGE
                line = partial[at : at + EDGE, :]
                face = j * FACE + a * EDGE
                if b == EDGE - 1:
                    line = line + ghosts[b_plus + face : b_plus + face + EDGE, :]
                if b == 0:
                    line = line + ghosts[b_minus + face : b_minus + face + EDGE, :]
                face = j * FACE + a * EDGE + b
                plus = ghosts[pl.ds(c_plus + face, EDGE, stride=0), :]
                minus = ghosts[pl.ds(c_minus + face, EDGE, stride=0), :]
                line = line + jnp.where(
                    c_at == EDGE - 1, plus, jnp.where(c_at == 0, minus, 0.0)
                )
                if j == count - 1 and a == EDGE - 1:
                    line = line + ghosts[a_plus + b * EDGE : a_plus + (b + 1) * EDGE, :]
                if j == 0 and a == 0:
                    line = line + ghosts[a_minus + b * EDGE : a_minus + (b + 1) * EDGE, :]
                lines.append(jnp.maximum(line, 0.0))
        block = jnp.concatenate(lines, 0)
        total[j * CELLS : (j + 1) * CELLS, :] = block
        hidden[j * CELLS : (j + 1) * CELLS, :] = block.astype(BF16)
    pack_faces(total, links, up, down)
    route(links[3, 4], up, down, first, second)


def lift_kernel(
    links,
    slots,
    block_levels,
    columns,
    partial,
    first_in,
    second_in,
    weights,
    height,
    *refs,
):
    *outs, ghosts, rows_in, sums, from_below, from_above = refs
    count = partial.shape[0] // CELLS
    ch = partial.shape[1]
    route(links[3, 4], first_in, second_in, from_above, from_below)
    ghost_terms(ghosts, from_below, from_above, links, weights)
    b_plus, b_minus, c_plus, c_minus, a_plus, a_minus = ghost_places(count)
    b_at = lax.rem(lax.broadcasted_iota(jnp.int32, (FACE, ch), 0), EDGE)

    def spread(to, j, c):
        rows = [to + (j * EDGE + a) * EDGE + c for a in range(EDGE)]
        return jnp.concatenate([ghosts[pl.ds(r, EDGE, stride=0), :] for r in rows], 0)

    for j in range(count):
        own = slice(j * FACE, (j + 1) * FACE)
        for c in range(EDGE):
            line = partial[pl.ds(j * CELLS + c, FACE, stride=EDGE), :]
            sides = jnp.where(b_at == 0, spread(b_minus, j, c), 0.0)
            line = line + jnp.where(b_at == EDGE - 1, spread(b_plus, j, c), sides)
            if c == EDGE - 1:
                line = line + ghosts[c_plus + j * FACE : c_plus + (j + 1) * FACE, :]
            if c == 0:
                line = line + ghosts[c_minus + j * FACE : c_minus + (j + 1) * FACE, :]
            if j == 0:
                low = line[0:EDGE] + ghosts[pl.ds(a_minus + c, EDGE, stride=EDGE), :]
                line = jnp.concatenate([low, line[EDGE:]], 0)
            if j == count - 1:
                high = line[FACE - EDGE :] + ghosts[pl.ds(a_plus + c, EDGE, stride=EDGE), :]
                line = jnp.concatenate([line[: FACE - EDGE], high], 0)
            rows_in[own, c * ch : (c + 1) * ch] = jnp.maximum(line, 0.0).astype(BF16)
    sums[...] = jnp.zeros_like(sums)

    def one(j, carry):
        rows = rows_in[pl.ds(pl.multiple_of(j * FACE, FACE), FACE), :]
        sums[slots[0, j]] += mm(rows, height[block_levels[0, j]])
        return carry

    lax.fori_loop(0, count, one, 0)
    peers = len(outs)
    per_peer = sums.shape[0] // peers
    row_at = lax.broadcasted_iota(jnp.int32, (ID_ROWS, LANES), 0)
    for k, out in enumerate(outs):
        ids = jnp.zeros(row_at.shape, F32)
        for i in range(per_peer):
            slot = (links[3, 7] ^ k) * per_peer + i
            block = sums[slot].astype(BF16)
            for h, lanes in halves(block.shape[1]):
                at = (h * per_peer + i) * FACE
                out[at : at + FACE, :] = block[:, lanes]
            ids = jnp.where(row_at == i, columns[0, slot].astype(F32), ids)
        out[out.shape[0] - ID_ROWS :, :] = ids.astype(BF16)


def gather_kernel(links, *refs):
    *arrived, bev, first, second, own, total, top, bottom = refs
    ch = bev.shape[1]
    parts = ch // LANES
    per_peer = (arrived[0].shape[0] - ID_ROWS) // (parts * FACE)
    total[...] = jnp.zeros_like(total)
    for source in arrived:
        ids = source[source.shape[0] - ID_ROWS :, :].astype(F32)
        for k in range(per_peer):
            column = jnp.max(ids[k : k + 1, :]).astype(jnp.int32)
            row_base = (column // TILE_BC) * (EDGE * COLS) + (column % TILE_BC) * EDGE
            for h in range(parts):
                start = (h * per_peer + k) * FACE
                block = source[start : start + FACE, :].astype(F32)
                for a in range(EDGE):
                    at = pl.multiple_of(row_base + a * COLS, EDGE)
                    total[h, pl.ds(at, EDGE), :] += block[a * EDGE : (a + 1) * EDGE, :]
    for h, lanes in halves(ch):
        bev[:, lanes] = total[h].astype(BF16)
        top[:, lanes] = total[h, 0 : HALO * COLS, :].astype(BF16)
        bottom[:, lanes] = total[h, (ROWS - HALO) * COLS :, :].astype(BF16)
        for x in range(HALO):
            far = COLS - HALO + x
            own[x, :, lanes] = total[h, pl.ds(x, ROWS, stride=COLS), :].astype(BF16)
            own[HALO + x, :, lanes] = total[h, pl.ds(far, ROWS, stride=COLS), :].astype(BF16)
    route(links[3, 6], bottom, top, first, second)


def halves(channels):
    return [(h, slice(h * LANES, (h + 1) * LANES)) for h in range(channels // LANES)]


WIDE_ROWS = ROWS + 2 * HALO
MID_ROWS = ROWS + HALO
RIM_ROWS = 72
INNER_ROWS = ROWS - 2
CORE_ROWS = ROWS - 4


def tap_columns(weights, dx):
    return jnp.concatenate([weights[dy * 3 + dx] for dy in range(3)], 0)


def three_rows(source, first_row, row_count):
    parts = []
    for dy in range(3):
        at = (first_row + dy) * COLS
        parts.append(source[at : at + row_count * COLS, :])
    return jnp.concatenate(parts, 1)


def clear(lines, side):
    at = lax.broadcasted_iota(jnp.int32, (1, EDGE, lines.shape[2]), 1)
    if side == 0:
        return jnp.concatenate([jnp.where(at == 0, 0.0, lines[:, :EDGE]), lines[:, EDGE:]], 1)
    inner = COLS - EDGE
    last = jnp.where(at == EDGE - 1, 0.0, lines[:, inner:])
    return jnp.concatenate([lines[:, :inner], last], 1)


def rows_conv(lhs, weights):
    count = lhs.shape[0]
    shape = (count // COLS, COLS, weights.shape[2])
    from_left = pltpu.roll(mm(lhs, tap_columns(weights, 0)), 1, 0)
    total = clear(from_left.reshape(shape), 0)
    total = total + mm(lhs, tap_columns(weights, 1)).reshape(shape)
    from_right = pltpu.roll(mm(lhs, tap_columns(weights, 2)), count - 1, 0)
    return total + clear(from_right.reshape(shape), 1)


def without_sides(lines):
    return clear(clear(lines, 0), 1)


def first_inner_kernel(bev, weights, inner):
    step = INNER_ROWS // 2
    for row in range(0, INNER_ROWS, step):
        block = jnp.maximum(rows_conv(three_rows(bev, row, step), weights), 0.0)
        block = without_sides(block).reshape(step * COLS, -1).astype(BF16)
        inner[row * COLS : (row + step) * COLS, :] = block


def strips(upper, lower):
    parts = []
    for source in (upper, lower):
        rows = [source[dy * COLS : (dy + HALO) * COLS] for dy in range(3)]
        parts.append(jnp.concatenate(rows, 1))
    return jnp.concatenate(parts, 0)


def second_core_kernel(
    links,
    inner,
    bev,
    first_row,
    second_row,
    weights_first,
    weights_second,
    out,
    flanks,
    ends,
    middle,
    above,
    below,
    sems,
):
    ch = bev.shape[1]
    two = HALO * COLS
    steps = 2
    step = CORE_ROWS // steps

    def store(lines, row, keep):
        count = lines.shape[0]
        keep[...] = lines.astype(BF16)
        for side, x in enumerate((0, COLS - EDGE)):
            flank = lines[:, x : x + EDGE, :].reshape(count * EDGE, ch)
            to = (side * ROWS + row) * EDGE
            for h, lanes in halves(ch):
                flanks[h, to : to + count * EDGE, :] = flank[:, lanes]

    copies = []
    for k in range(steps):
        row = k * step + HALO
        lines = rows_conv(three_rows(inner, k * step, step), weights_second)
        own = bev[row * COLS : (row + step) * COLS, :].astype(F32)
        kept = middle.at[k * step : (k + 1) * step]
        store(lines + own.reshape(lines.shape), row, kept)
        copies.append(pltpu.make_async_copy(kept, out.at[row : row + step], sems.at[k]))
        copies[-1].start()

    route(links[3, 6], first_row, second_row, below, above)
    top, bottom = bev[0:two, :], bev[ROWS * COLS - two :, :]
    high = jnp.concatenate([above[...], top], 0)
    low = jnp.concatenate([bottom, below[...]], 0)
    strip = without_sides(jnp.maximum(rows_conv(strips(high, low), weights_first), 0.0))
    line = lax.broadcasted_iota(jnp.int32, strip.shape, 0)
    keep = jnp.where(line == 0, links[3, 0], jnp.where(line == 3, links[3, 1], 1)).astype(F32)
    strip = (strip * keep).reshape(2 * two, ch).astype(BF16)

    high = jnp.concatenate([strip[0:two], inner[0:two, :]], 0)
    low = jnp.concatenate([inner[INNER_ROWS * COLS - two :, :], strip[two:]], 0)
    lines = rows_conv(strips(high, low), weights_second)
    own = jnp.concatenate([top, bottom], 0).astype(F32)
    lines = lines + own.reshape(lines.shape)
    store(lines[0:HALO], 0, ends.at[0:HALO])
    store(lines[HALO:], ROWS - HALO, ends.at[HALO:])
    for copy in copies:
        copy.wait()


def edges_kernel(
    links,
    unused,
    flanks,
    ends,
    own_left,
    own_right,
    first_in,
    second_in,
    weights_first,
    weights_second,
    out,
    sides,
    total,
    edge,
    sems,
):
    ch = out.shape[2]
    sides[:, WIDE_ROWS:, :] = jnp.zeros_like(sides[:, WIDE_ROWS:, :])

    def place(base, source):
        for x in range(HALO):
            sides[base + x, 0:WIDE_ROWS, :] = source[x, :, :].astype(F32)

    place(2, own_left)
    place(4, own_right)

    @pl.when(links[3, 5] == 0)
    def _():
        place(0, second_in)
        place(6, first_in)

    @pl.when(links[3, 5] != 0)
    def _():
        place(0, first_in)
        place(6, second_in)

    inner_columns = slice(EDGE, COLS - EDGE)
    copies = []
    for k, (row, source) in enumerate(((0, 0), (ROWS - HALO, HALO))):
        kept = ends.at[source : source + HALO, inner_columns, :]
        to = out.at[row : row + HALO, inner_columns, :]
        copies.append(pltpu.make_async_copy(kept, to, sems.at[k]))
        copies[-1].start()
    tall = sides.shape[1]
    total[...] = flanks[...]
    narrow = [sides[k, :, :].astype(BF16) for k in range(8)]
    lhs = [jnp.concatenate(narrow[start : start + 3], 1) for start in (0, 1, 4, 5)]
    lhs = jnp.concatenate(lhs, 0)
    taps = []
    for dy in range(3):
        rows = [weights_first[dy * 3 + dx] for dx in range(3)]
        taps.append(mm(lhs, jnp.concatenate(rows, 0)))
    row_at = lax.broadcasted_iota(jnp.int32, (RIM_ROWS, ch), 0)
    keep = jnp.where(row_at == MID_ROWS - 1, links[3, 1], 1)
    keep = jnp.where(row_at == 0, links[3, 0], keep).astype(F32)
    column = []
    for k, side_keep in enumerate((links[3, 2], None, None, links[3, 3])):
        at = k * tall
        block = sum(taps[dy][at + dy : at + dy + RIM_ROWS, :] for dy in range(3))
        block = jnp.maximum(block, 0.0) * keep
        if side_keep is not None:
            block = block * side_keep.astype(F32)
        zeros = jnp.zeros((tall - RIM_ROWS, ch), F32)
        column.append(jnp.concatenate([block, zeros], 0).astype(BF16))

    parts = []
    for dx, pair in enumerate(((0, 1), (1, 2), (2, 3))):
        lhs = jnp.concatenate([column[k] for k in pair], 0)
        taps = [mm(lhs, weights_second[dy * 3 + dx]) for dy in range(3)]
        for at in (0, tall):
            parts.append(sum(taps[dy][at + dy : at + dy + ROWS, :] for dy in range(3)))
    added = (
        (0, parts[0] + parts[2]),
        (1, parts[1]),
        (ROWS * EDGE + EDGE - 2, parts[4]),
        (ROWS * EDGE + EDGE - 1, parts[3] + parts[5]),
    )
    for at, block in added:
        for h, lanes in halves(ch):
            total[h, pl.ds(at, ROWS, stride=EDGE), :] += block[:, lanes]
    for side, x in enumerate((0, COLS - EDGE)):
        group = slice(side * ROWS * EDGE, (side + 1) * ROWS * EDGE)
        for h, lanes in halves(ch):
            edge[side, :, :, lanes] = total[h, group, :].reshape(ROWS, EDGE, LANES).astype(BF16)
        copies.append(
            pltpu.make_async_copy(edge.at[side], out.at[:, x : x + EDGE, :], sems.at[2 + side])
        )
        copies[-1].start()
    for copy in copies:
        copy.wait()


def call(kernel, out_shape, scalars, arrays, scratch=(), mib=12):
    multiple = isinstance(out_shape, (list, tuple))
    return pl.pallas_call(
        kernel,
        out_shape=out_shape,
        in_specs=[SMEM] * len(scalars) + [VMEM] * len(arrays),
        out_specs=[VMEM] * len(out_shape) if multiple else VMEM,
        scratch_shapes=list(scratch),
        compiler_params=pltpu.CompilerParams(vmem_limit_bytes=mib << 20),
    )(*scalars, *arrays)


def local(
    features,
    links,
    block_slot,
    block_level,
    slot_column,
    conv_first,
    conv_second,
    height_w,
    plane_first,
    plane_second,
):
    count, _, ch = features.shape
    rows = count * CELLS
    faces = (2 * count + 1) * FACE
    mapped = plane_first.shape[3]
    peers = lax.axis_size("gx")
    slot_total = slot_column.shape[1]
    per_peer = slot_total // peers
    x = features.reshape(rows, ch)
    w_first = conv_first.reshape(-1, ch)
    w_second = conv_second.reshape(-1, ch)
    k_first = plane_first.reshape(9, mapped, mapped)
    k_second = plane_second.reshape(9, mapped, mapped)
    slots = block_slot.reshape(1, count)
    block_levels = block_level.reshape(1, count)
    both = ("gy", "gx")

    face_shape = jax.ShapeDtypeStruct((faces, ch), BF16)
    wide = pltpu.VMEM((rows, ch), F32)
    part_shape = jax.ShapeDtypeStruct((rows, ch), F32)

    gy, gx = lax.axis_index("gy"), lax.axis_index("gx")
    last_y = lax.axis_size("gy") - 1
    places = [gy > 0, gy < last_y, gx > 0, gx < peers - 1, lax.axis_index(both) % 2, gx % 2, gy % 2, gx]
    lane = lax.broadcasted_iota(jnp.int32, (1, count), 1)
    flags = sum(jnp.where(lane == k, jnp.int32(v), 0) for k, v in enumerate(places))
    links = jnp.concatenate([links.T, flags], 0)
    face = pltpu.VMEM((faces, ch), BF16)
    ghosts = pltpu.VMEM((2 * faces, ch), F32)
    first, second = call(pack_kernel, (face_shape, face_shape), (links,), (x,), (wide, face, face))
    first, second = swap(first, second, both)
    partial = call(first_interior_kernel, part_shape, (links,), (x, w_first))
    hidden, first, second = call(
        hidden_kernel,
        (jax.ShapeDtypeStruct((rows, ch), BF16), face_shape, face_shape),
        (links,),
        (partial, first, second, w_first),
        (wide, face, face, face, face, ghosts),
    )
    first, second = swap(first, second, both)
    partial = call(second_interior_kernel, part_shape, (links,), (hidden, x, w_second))
    payload = (mapped // LANES * per_peer * FACE + ID_ROWS, LANES)
    outgoing = call(
        lift_kernel,
        [jax.ShapeDtypeStruct(payload, BF16)] * peers,
        (links, slots, block_levels, slot_column),
        (partial, first, second, w_second, height_w),
        (
            ghosts,
            pltpu.VMEM((count * FACE, EDGE * ch), BF16),
            pltpu.VMEM((slot_total, FACE, mapped), F32),
            face,
            face,
        ),
    )
    arrived = list(outgoing)
    for k in trade_order(peers):
        arrived[k] = lax.ppermute(outgoing[k], "gx", [(i, i ^ k) for i in range(peers)])

    row_shape = jax.ShapeDtypeStruct((HALO * COLS, mapped), BF16)
    row = pltpu.VMEM((HALO * COLS, mapped), BF16)
    bev, first, second, own = call(
        gather_kernel,
        (
            jax.ShapeDtypeStruct((ROWS * COLS, mapped), BF16),
            row_shape,
            row_shape,
            jax.ShapeDtypeStruct((2 * HALO, ROWS, mapped), BF16),
        ),
        (links,),
        arrived,
        (pltpu.VMEM((mapped // LANES, ROWS * COLS, LANES), F32), row, row),
    )
    first_row, second_row = swap(first, second, "gy")
    inner = call(
        first_inner_kernel,
        jax.ShapeDtypeStruct((INNER_ROWS * COLS, mapped), BF16),
        (),
        (bev, k_first),
    )
    first_row, second_row, inner = lax.optimization_barrier((first_row, second_row, inner))
    odd_y, odd_x = gy % 2 == 1, gx % 2 == 1
    corner_above = jnp.where(odd_y, first_row, second_row).reshape(HALO, COLS, mapped)
    corner_below = jnp.where(odd_y, second_row, first_row).reshape(HALO, COLS, mapped)

    def side(own, at):
        return jnp.concatenate(
            [
                corner_above[:, at : at + HALO].transpose(1, 0, 2),
                own,
                corner_below[:, at : at + HALO].transpose(1, 0, 2),
            ],
            1,
        )

    own_left, own_right = side(own[:HALO], 0), side(own[HALO:], COLS - HALO)
    first, second = swap(
        jnp.where(odd_x, own_left, own_right), jnp.where(odd_x, own_right, own_left), "gx"
    )
    flank = (mapped // LANES, 2 * ROWS * EDGE, LANES)
    out_shape = jax.ShapeDtypeStruct((ROWS, COLS, mapped), BF16)
    limit = pltpu.CompilerParams(vmem_limit_bytes=12 << 20)
    out, flanks, ends = pl.pallas_call(
        second_core_kernel,
        name="second_core",
        out_shape=(
            out_shape,
            jax.ShapeDtypeStruct(flank, F32),
            jax.ShapeDtypeStruct((2 * HALO, COLS, mapped), BF16),
        ),
        in_specs=[SMEM] + [VMEM] * 6,
        out_specs=[ANY, VMEM, VMEM],
        scratch_shapes=[
            pltpu.VMEM((CORE_ROWS, COLS, mapped), BF16),
            row,
            row,
            pltpu.SemaphoreType.DMA((2,)),
        ],
        compiler_params=limit,
    )(links, inner, bev, first_row, second_row, k_first, k_second)
    return pl.pallas_call(
        edges_kernel,
        name="edges",
        out_shape=out_shape,
        in_specs=[SMEM, ANY] + [VMEM] * 8,
        out_specs=ANY,
        scratch_shapes=[
            pltpu.VMEM((8, RIM_ROWS + EDGE, mapped), F32),
            pltpu.VMEM(flank, F32),
            pltpu.VMEM((2, ROWS, EDGE, mapped), BF16),
            pltpu.SemaphoreType.DMA((4,)),
        ],
        input_output_aliases={1: 0},
        compiler_params=limit,
    )(links, out, flanks, ends, own_left, own_right, first, second, k_first, k_second)


def solution(mesh):
    in_specs = (
        P(("gy", "gx"), None, None),
        P(("gy", "gx"), None),
        P(("gy", "gx")),
        P(("gy", "gx")),
        P(("gy", "gx"), None),
        P(),
        P(),
        P(),
        P(),
        P(),
    )
    out_specs = P("gy", "gx", None)

    return jax.shard_map(local, mesh=mesh, in_specs=in_specs, out_specs=out_specs, check_vma=False)
```

profile of v0, /device:TPU:9, one launch (start us, length us, event | category | flops | bytes accessed | tf_op | source)
XLA Modules:
  0.0 71.5 jit_solution(6766587818454193692)
XLA Ops:
  0.7 1.2 %copy-done.1 = bf16[8,512,128]{2,1,0:T(8,128)(2,1)S(1)} copy-done((bf16[8,512,128]{2,1,0:T(8,128)(2,1)S(1)}, bf16[8,512,128]{2,1,0:T(8,128)(2,1)}, u32[]{:S(2)}) %copy-start.1) | copy-done | bytes 1048600
  2.9 1.3 %collective-permute-start = (bf16[1088,128]{1,0:T(8,128)(2,1)S(1)}, bf16[1088,128]{1,0:T(8,128)(2,1)S(1)}, u32[]{:S(2)}, u32[]{:S(2)}) collective-permute-start(bf16[1088,128]{1,0:T(8,128)(2,1)S(1)} %get-tuple-element.28), channel_id=1, source_target_pairs={{0,1},{1,0},{2,3},{3,2},{4,5},{5,4},{6,7},{7,6},{8,9},{9,8},{10,11... | collective-permute-start | bytes 835592 | tf_op jit(solution)/shard_map/ppermute | solution.py:32
  4.2 1.9 %collective-permute-start.1 = (bf16[1088,128]{1,0:T(8,128)(2,1)S(1)}, bf16[1088,128]{1,0:T(8,128)(2,1)S(1)}, u32[]{:S(2)}, u32[]{:S(2)}) collective-permute-start(bf16[1088,128]{1,0:T(8,128)(2,1)S(1)} %get-tuple-element.29), channel_id=1, source_target_pairs={{1,2},{2,1},{3,4},{4,3},{5,6},{6,5},{7,8},{8,7},{9,10},{10,9},{11,... | collective-permute-start | bytes 835592 | tf_op jit(solution)/shard_map/ppermute | solution.py:33
  7.0 3.8 %shard_map.100.partial = f32[4096,128]{1,0:T(8,128)S(1)} custom-call(s32[4,8]{1,0:T(4,128)S(1)} %pad_add_fusion.links, bf16[4096,128]{1,0:T(8,128)(2,1)S(1)} %bitcast.22, bf16[896,128]{1,0:T(8,128)(2,1)S(1)} %bitcast.26), custom_call_target="tpu_custom_call" | custom-call | tf_op jit(solution)/shard_map/pallas_call | solution.py:528
  10.8 5.6 %collective-permute-done.first_in = bf16[1088,128]{1,0:T(8,128)(2,1)S(1)} collective-permute-done((bf16[1088,128]{1,0:T(8,128)(2,1)S(1)}, bf16[1088,128]{1,0:T(8,128)(2,1)S(1)}, u32[]{:S(2)}, u32[]{:S(2)}) %collective-permute-start) | collective-permute-done | bytes 278560 | tf_op jit(solution)/shard_map/ppermute | solution.py:32
  16.5 1.4 %shard_map.102 = (bf16[4096,128]{1,0:T(8,128)(2,1)S(1)}, bf16[1088,128]{1,0:T(8,128)(2,1)S(1)}, bf16[1088,128]{1,0:T(8,128)(2,1)S(1)}) custom-call(s32[4,8]{1,0:T(4,128)S(1)} %pad_add_fusion.links, f32[4096,128]{1,0:T(8,128)S(1)} %shard_map.100.partial, bf16[1088,128]{1,0:T(8,128)(2,1)S(1)} %collective-permute-done.first_in, ...), custom_call_target="tpu_custom_call" | custom-call | tf_op jit(solution)/shard_map/pallas_call | solution.py:528
  17.9 1.3 %collective-permute-start.2 = (bf16[1088,128]{1,0:T(8,128)(2,1)S(1)}, bf16[1088,128]{1,0:T(8,128)(2,1)S(1)}, u32[]{:S(2)}, u32[]{:S(2)}) collective-permute-start(bf16[1088,128]{1,0:T(8,128)(2,1)S(1)} %get-tuple-element.31), channel_id=1, source_target_pairs={{0,1},{1,0},{2,3},{3,2},{4,5},{5,4},{6,7},{7,6},{8,9},{9,8},{10,11... | collective-permute-start | bytes 835592 | tf_op jit(solution)/shard_map/ppermute | solution.py:32
  19.2 2.0 %collective-permute-start.3 = (bf16[1088,128]{1,0:T(8,128)(2,1)S(1)}, bf16[1088,128]{1,0:T(8,128)(2,1)S(1)}, u32[]{:S(2)}, u32[]{:S(2)}) collective-permute-start(bf16[1088,128]{1,0:T(8,128)(2,1)S(1)} %get-tuple-element.32), channel_id=1, source_target_pairs={{1,2},{2,1},{3,4},{4,3},{5,6},{6,5},{7,8},{8,7},{9,10},{10,9},{11,... | collective-permute-start | bytes 835592 | tf_op jit(solution)/shard_map/ppermute | solution.py:33
  21.3 3.8 %shard_map.103.partial = f32[4096,128]{1,0:T(8,128)S(1)} custom-call(s32[4,8]{1,0:T(4,128)S(1)} %pad_add_fusion.links, bf16[4096,128]{1,0:T(8,128)(2,1)S(1)} %get-tuple-element.30.hidden, bf16[4096,128]{1,0:T(8,128)(2,1)S(1)} %bitcast.23, bf16[896,128]{1,0:T(8,128)(2,1)S(1)} %bitcast.28), custom_call_target="tpu_custom_call" | custom-call | tf_op jit(solution)/shard_map/pallas_call | solution.py:528
  25.1 4.5 %collective-permute-done.2.first_in = bf16[1088,128]{1,0:T(8,128)(2,1)S(1)} collective-permute-done((bf16[1088,128]{1,0:T(8,128)(2,1)S(1)}, bf16[1088,128]{1,0:T(8,128)(2,1)S(1)}, u32[]{:S(2)}, u32[]{:S(2)}) %collective-permute-start.2) | collective-permute-done | bytes 278560 | tf_op jit(solution)/shard_map/ppermute | solution.py:32
  29.7 3.3 %shard_map.104 = (bf16[264,128]{1,0:T(8,128)(2,1)S(1)}, bf16[264,128]{1,0:T(8,128)(2,1)S(1)}, bf16[264,128]{1,0:T(8,128)(2,1)S(1)}, bf16[264,128]{1,0:T(8,128)(2...) custom-call(s32[4,8]{1,0:T(4,128)S(1)} %pad_add_fusion.links, ...), custom_call_target="tpu_custom_call" | custom-call | tf_op jit(solution)/shard_map/pallas_call | solution.py:528
  33.0 2.3 %collective-permute-start.4 = (bf16[264,128]{1,0:T(8,128)(2,1)S(1)}, bf16[264,128]{1,0:T(8,128)(2,1)S(1)}, u32[]{:S(2)}, u32[]{:S(2)}) collective-permute-start(bf16[264,128]{1,0:T(8,128)(2,1)S(1)} %get-tuple-element.34), channel_id=1, source_target_pairs={{0,1},{1,0},{2,3},{3,2},{4,5},{5,4},{6,7},{7,6},{8,9},{9,8},{10,11... | collective-permute-start | bytes 202760 | tf_op jit(solution)/shard_map/ppermute | solution.py:606
  36.6 4.6 %collective-permute-start.7 = (bf16[264,128]{1,0:T(8,128)(2,1)S(1)}, bf16[264,128]{1,0:T(8,128)(2,1)S(1)}, u32[]{:S(2)}, u32[]{:S(2)}) collective-permute-start(bf16[264,128]{1,0:T(8,128)(2,1)S(1)} %get-tuple-element.37), channel_id=1, source_target_pairs={{0,4},{1,5},{2,6},{3,7},{4,0},{5,1},{6,2},{7,3},{8,12},{9,13},{10,... | collective-permute-start | bytes 202760 | tf_op jit(solution)/shard_map/ppermute | solution.py:606
  42.3 1.2 %collective-permute-start.9 = (bf16[264,128]{1,0:T(8,128)(2,1)S(1)}, bf16[264,128]{1,0:T(8,128)(2,1)S(1)}, u32[]{:S(2)}, u32[]{:S(2)}) collective-permute-start(bf16[264,128]{1,0:T(8,128)(2,1)S(1)} %get-tuple-element.39), channel_id=1, source_target_pairs={{0,6},{1,7},{2,4},{3,5},{4,2},{5,3},{6,0},{7,1},{8,14},{9,15},{10,... | collective-permute-start | bytes 202760 | tf_op jit(solution)/shard_map/ppermute | solution.py:606
  43.8 1.7 %collective-permute-done.7.refs_4_ = bf16[264,128]{1,0:T(8,128)(2,1)S(1)} collective-permute-done((bf16[264,128]{1,0:T(8,128)(2,1)S(1)}, bf16[264,128]{1,0:T(8,128)(2,1)S(1)}, u32[]{:S(2)}, u32[]{:S(2)}) %collective-permute-start.7) | collective-permute-done | bytes 67616 | tf_op jit(solution)/shard_map/ppermute | solution.py:606
  45.5 4.3 %collective-permute-done.8.refs_5_ = bf16[264,128]{1,0:T(8,128)(2,1)S(1)} collective-permute-done((bf16[264,128]{1,0:T(8,128)(2,1)S(1)}, bf16[264,128]{1,0:T(8,128)(2,1)S(1)}, u32[]{:S(2)}, u32[]{:S(2)}) %collective-permute-start.8) | collective-permute-done | bytes 67616 | tf_op jit(solution)/shard_map/ppermute | solution.py:606
  49.8 1.6 %collective-permute-done.9.refs_6_ = bf16[264,128]{1,0:T(8,128)(2,1)S(1)} collective-permute-done((bf16[264,128]{1,0:T(8,128)(2,1)S(1)}, bf16[264,128]{1,0:T(8,128)(2,1)S(1)}, u32[]{:S(2)}, u32[]{:S(2)}) %collective-permute-start.9) | collective-permute-done | bytes 67616 | tf_op jit(solution)/shard_map/ppermute | solution.py:606
  51.4 3.0 %collective-permute-done.10.refs_7_ = bf16[264,128]{1,0:T(8,128)(2,1)S(1)} collective-permute-done((bf16[264,128]{1,0:T(8,128)(2,1)S(1)}, bf16[264,128]{1,0:T(8,128)(2,1)S(1)}, u32[]{:S(2)}, u32[]{:S(2)}) %collective-permute-start.10) | collective-permute-done | bytes 67616 | tf_op jit(solution)/shard_map/ppermute | solution.py:606
  54.4 1.3 %shard_map.105 = (bf16[2048,256]{1,0:T(8,128)(2,1)S(1)}, bf16[64,256]{1,0:T(8,128)(2,1)S(1)}, bf16[64,256]{1,0:T(8,128)(2,1)S(1)}, bf16[4,64,256]{2,1,0:T(8,128)(2,1)S(1)}) custom-call(s32[4,8]{1,0:T(4,128)S(1)} %pad_add_fusion.links, bf16[264,128]{1,0:T(8,128)(2,1)S(1)} %get-tuple-element.33.refs_0_, bf16[264,128]{1,0:T(8,128)(2,1)S(1)} %collective-permute-done.4.refs_1_, ...), custom_call_target="tpu_custom_call" | custom-call | tf_op jit(solution)/shard_map/pallas_call | solution.py:528
  56.6 1.9 %collective-permute-start.12 = (bf16[64,256]{1,0:T(8,128)(2,1)S(1)}, bf16[64,256]{1,0:T(8,128)(2,1)S(1)}, u32[]{:S(2)}, u32[]{:S(2)}) collective-permute-start(bf16[64,256]{1,0:T(8,128)(2,1)S(1)} %get-tuple-element.42), channel_id=1, source_target_pairs={{8,16},{16,8},{9,17},{17,9},{10,18},{18,10},{11,19},{19,11},{12,20... | collective-permute-start | bytes 98312 | tf_op jit(solution)/shard_map/ppermute | solution.py:33
  58.5 2.5 %shard_map.106.inner = bf16[1984,256]{1,0:T(8,128)(2,1)S(1)} custom-call(bf16[2048,256]{1,0:T(8,128)(2,1)S(1)} %get-tuple-element.43.bev, bf16[9,256,256]{2,1,0:T(8,128)(2,1)S(1)} %bitcast.18), custom_call_target="tpu_custom_call" | custom-call | tf_op jit(solution)/shard_map/pallas_call | solution.py:528
  62.5 2.6 %collective-permute-start.14 = (bf16[2,68,256]{2,1,0:T(8,128)(2,1)S(1)}, bf16[2,68,256]{2,1,0:T(8,128)(2,1)S(1)}, u32[]{:S(2)}, u32[]{:S(2)}) collective-permute-start(bf16[2,68,256]{2,1,0:T(8,128)(2,1)S(1)} %get-tuple-element.51), channel_id=1, source_target_pairs={{1,2},{2,1},{3,4},{4,3},{5,6},{6,5},{9,10},{10,9},{11,12},{12,11},... | collective-permute-start | bytes 208904 | tf_op jit(solution)/shard_map/ppermute | solution.py:33
  65.1 3.8 %second_core.1 = (bf16[64,32,256]{2,1,0:T(8,128)(2,1)}, f32[2,1024,128]{2,1,0:T(8,128)S(1)}, bf16[4,32,256]{2,1,0:T(8,128)(2,1)S(1)}) custom-call(s32[4,8]{1,0:T(4,128)S(1)} %pad_add_fusion.links, bf16[1984,256]{1,0:T(8,128)(2,1)S(1)} %shard_map.106.inner, bf16[2048,256]{1,0:T(8,128)(2,1)S(1)} %get-tuple-element.43.bev, ...), custom_call_target="tpu_custom_call" | custom-call | tf_op jit(solution)/shard_map/second_core/pallas_call | solution.py:651
  69.0 2.5 %edges.1 = bf16[64,32,256]{2,1,0:T(8,128)(2,1)} custom-call(s32[4,8]{1,0:T(4,128)S(1)} %pad_add_fusion.links, bf16[64,32,256]{2,1,0:T(8,128)(2,1)} %get-tuple-element.47.unused, f32[2,1024,128]{2,1,0:T(8,128)S(1)} %get-tuple-element.48.flanks, bf16[4,32,256]{2,1,0:T(8,128)(2,1)S(1)} %get-tuple-element.49.ends, ...), custom_call_target="tpu_custom_call", output_to_operand_aliasing={{}: (1, {})} | custom-call | tf_op jit(solution)/shard_map/edges/pallas_call | solution.py:669
  (44 shorter events, 7.6 us)
Async XLA Ops:
  0.7 1.2 %copy-start.1 = (bf16[8,512,128]{2,1,0:T(8,128)(2,1)S(1)}, bf16[8,512,128]{2,1,0:T(8,128)(2,1)}, u32[]{:S(2)}) copy-start(bf16[8,512,128]{2,1,0:T(8,128)(2,1)} %param.10) | copy-start | bytes 3145732
  2.9 13.6 %collective-permute-start = (bf16[1088,128]{1,0:T(8,128)(2,1)S(1)}, bf16[1088,128]{1,0:T(8,128)(2,1)S(1)}, u32[]{:S(2)}, u32[]{:S(2)}) collective-permute-start(bf16[1088,128]{1,0:T(8,128)(2,1)S(1)} %get-tuple-element.28), channel_id=1, source_target_pairs={{0,1},{1,0},{2,3},{3,2},{4,5},{5,4},{6,7},{7,6},{8,9},{9,8},{10,11... | collective-permute-start | bytes 835592 | tf_op jit(solution)/shard_map/ppermute | solution.py:32
  4.2 12.3 %collective-permute-start.1 = (bf16[1088,128]{1,0:T(8,128)(2,1)S(1)}, bf16[1088,128]{1,0:T(8,128)(2,1)S(1)}, u32[]{:S(2)}, u32[]{:S(2)}) collective-permute-start(bf16[1088,128]{1,0:T(8,128)(2,1)S(1)} %get-tuple-element.29), channel_id=1, source_target_pairs={{1,2},{2,1},{3,4},{4,3},{5,6},{6,5},{7,8},{8,7},{9,10},{10,9},{11,... | collective-permute-start | bytes 835592 | tf_op jit(solution)/shard_map/ppermute | solution.py:33
  10.8 10.4 %copy-start.2 = (bf16[8,512,128]{2,1,0:T(8,128)(2,1)S(1)}, bf16[8,512,128]{2,1,0:T(8,128)(2,1)}, u32[]{:S(2)}) copy-start(bf16[8,512,128]{2,1,0:T(8,128)(2,1)} %param.10) | copy-start | bytes 3145732
  10.8 10.4 %copy-start.6 = (bf16[7,128,128]{2,1,0:T(8,128)(2,1)S(1)}, bf16[7,128,128]{2,1,0:T(8,128)(2,1)}, u32[]{:S(2)}) copy-start(bf16[7,128,128]{2,1,0:T(8,128)(2,1)} %param.16) | copy-start | bytes 688132
  17.9 11.7 %collective-permute-start.2 = (bf16[1088,128]{1,0:T(8,128)(2,1)S(1)}, bf16[1088,128]{1,0:T(8,128)(2,1)S(1)}, u32[]{:S(2)}, u32[]{:S(2)}) collective-permute-start(bf16[1088,128]{1,0:T(8,128)(2,1)S(1)} %get-tuple-element.31), channel_id=1, source_target_pairs={{0,1},{1,0},{2,3},{3,2},{4,5},{5,4},{6,7},{7,6},{8,9},{9,8},{10,11... | collective-permute-start | bytes 835592 | tf_op jit(solution)/shard_map/ppermute | solution.py:32
  19.2 10.5 %collective-permute-start.3 = (bf16[1088,128]{1,0:T(8,128)(2,1)S(1)}, bf16[1088,128]{1,0:T(8,128)(2,1)S(1)}, u32[]{:S(2)}, u32[]{:S(2)}) collective-permute-start(bf16[1088,128]{1,0:T(8,128)(2,1)S(1)} %get-tuple-element.32), channel_id=1, source_target_pairs={{1,2},{2,1},{3,4},{4,3},{5,6},{6,5},{7,8},{8,7},{9,10},{10,9},{11,... | collective-permute-start | bytes 835592 | tf_op jit(solution)/shard_map/ppermute | solution.py:33
  21.3 8.4 %copy-start.4 = (bf16[4,1024,256]{2,1,0:T(8,128)(2,1)S(1)}, bf16[4,1024,256]{2,1,0:T(8,128)(2,1)}, u32[]{:S(2)}) copy-start(bf16[4,1024,256]{2,1,0:T(8,128)(2,1)} %height.1) | copy-start | bytes 6291460
  21.3 8.4 %copy-start.7 = (s32[8]{0:T(128)S(1)}, s32[8]{0:T(128)}, u32[]{:S(2)}) copy-start(s32[8]{0:T(128)} %param.12) | copy-start | bytes 100
  21.3 8.4 %copy-start.8 = (s32[8]{0:T(128)S(1)}, s32[8]{0:T(128)}, u32[]{:S(2)}) copy-start(s32[8]{0:T(128)} %param.13) | copy-start | bytes 100
  21.3 8.4 %copy-start.9 = (s32[1,16]{1,0:T(1,128)S(1)}, s32[1,16]{1,0:T(1,128)}, u32[]{:S(2)}) copy-start(s32[1,16]{1,0:T(1,128)} %columns.1) | copy-start | bytes 196
  29.7 28.8 %copy-start = (bf16[3,3,256,256]{3,2,1,0:T(8,128)(2,1)S(1)}, bf16[3,3,256,256]{3,2,1,0:T(8,128)(2,1)}, u32[]{:S(2)}) copy-start(bf16[3,3,256,256]{3,2,1,0:T(8,128)(2,1)} %param.18) | copy-start | bytes 3538948
  33.0 9.3 %collective-permute-start.4 = (bf16[264,128]{1,0:T(8,128)(2,1)S(1)}, bf16[264,128]{1,0:T(8,128)(2,1)S(1)}, u32[]{:S(2)}, u32[]{:S(2)}) collective-permute-start(bf16[264,128]{1,0:T(8,128)(2,1)S(1)} %get-tuple-element.34), channel_id=1, source_target_pairs={{0,1},{1,0},{2,3},{3,2},{4,5},{5,4},{6,7},{7,6},{8,9},{9,8},{10,11... | collective-permute-start | bytes 202760 | tf_op jit(solution)/shard_map/ppermute | solution.py:606
  35.3 8.2 %collective-permute-start.5 = (bf16[264,128]{1,0:T(8,128)(2,1)S(1)}, bf16[264,128]{1,0:T(8,128)(2,1)S(1)}, u32[]{:S(2)}, u32[]{:S(2)}) collective-permute-start(bf16[264,128]{1,0:T(8,128)(2,1)S(1)} %get-tuple-element.35), channel_id=1, source_target_pairs={{0,2},{1,3},{2,0},{3,1},{4,6},{5,7},{6,4},{7,5},{8,10},{9,11},{10,... | collective-permute-start | bytes 202760 | tf_op jit(solution)/shard_map/ppermute | solution.py:606
  35.5 8.3 %collective-permute-start.6 = (bf16[264,128]{1,0:T(8,128)(2,1)S(1)}, bf16[264,128]{1,0:T(8,128)(2,1)S(1)}, u32[]{:S(2)}, u32[]{:S(2)}) collective-permute-start(bf16[264,128]{1,0:T(8,128)(2,1)S(1)} %get-tuple-element.36), channel_id=1, source_target_pairs={{0,3},{1,2},{2,1},{3,0},{4,7},{5,6},{6,5},{7,4},{8,11},{9,10},{10,... | collective-permute-start | bytes 202760 | tf_op jit(solution)/shard_map/ppermute | solution.py:606
  36.6 8.9 %collective-permute-start.7 = (bf16[264,128]{1,0:T(8,128)(2,1)S(1)}, bf16[264,128]{1,0:T(8,128)(2,1)S(1)}, u32[]{:S(2)}, u32[]{:S(2)}) collective-permute-start(bf16[264,128]{1,0:T(8,128)(2,1)S(1)} %get-tuple-element.37), channel_id=1, source_target_pairs={{0,4},{1,5},{2,6},{3,7},{4,0},{5,1},{6,2},{7,3},{8,12},{9,13},{10,... | collective-permute-start | bytes 202760 | tf_op jit(solution)/shard_map/ppermute | solution.py:606
  41.2 8.6 %collective-permute-start.8 = (bf16[264,128]{1,0:T(8,128)(2,1)S(1)}, bf16[264,128]{1,0:T(8,128)(2,1)S(1)}, u32[]{:S(2)}, u32[]{:S(2)}) collective-permute-start(bf16[264,128]{1,0:T(8,128)(2,1)S(1)} %get-tuple-element.38), channel_id=1, source_target_pairs={{0,5},{1,4},{2,7},{3,6},{4,1},{5,0},{6,3},{7,2},{8,13},{9,12},{10,... | collective-permute-start | bytes 202760 | tf_op jit(solution)/shard_map/ppermute | solution.py:606
  42.3 9.1 %collective-permute-start.9 = (bf16[264,128]{1,0:T(8,128)(2,1)S(1)}, bf16[264,128]{1,0:T(8,128)(2,1)S(1)}, u32[]{:S(2)}, u32[]{:S(2)}) collective-permute-start(bf16[264,128]{1,0:T(8,128)(2,1)S(1)} %get-tuple-element.39), channel_id=1, source_target_pairs={{0,6},{1,7},{2,4},{3,5},{4,2},{5,3},{6,0},{7,1},{8,14},{9,15},{10,... | collective-permute-start | bytes 202760 | tf_op jit(solution)/shard_map/ppermute | solution.py:606
  43.5 10.9 %collective-permute-start.10 = (bf16[264,128]{1,0:T(8,128)(2,1)S(1)}, bf16[264,128]{1,0:T(8,128)(2,1)S(1)}, u32[]{:S(2)}, u32[]{:S(2)}) collective-permute-start(bf16[264,128]{1,0:T(8,128)(2,1)S(1)} %get-tuple-element.40), channel_id=1, source_target_pairs={{0,7},{1,6},{2,5},{3,4},{4,3},{5,2},{6,1},{7,0},{8,15},{9,14},{10,... | collective-permute-start | bytes 202760 | tf_op jit(solution)/shard_map/ppermute | solution.py:606
  55.7 9.4 %copy-start.3 = (bf16[3,3,256,256]{3,2,1,0:T(8,128)(2,1)S(1)}, bf16[3,3,256,256]{3,2,1,0:T(8,128)(2,1)}, u32[]{:S(2)}) copy-start(bf16[3,3,256,256]{3,2,1,0:T(8,128)(2,1)} %param.19) | copy-start | bytes 3538948
  55.7 5.4 %collective-permute-start.11 = (bf16[64,256]{1,0:T(8,128)(2,1)S(1)}, bf16[64,256]{1,0:T(8,128)(2,1)S(1)}, u32[]{:S(2)}, u32[]{:S(2)}) collective-permute-start(bf16[64,256]{1,0:T(8,128)(2,1)S(1)} %get-tuple-element.41), channel_id=1, source_target_pairs={{0,8},{8,0},{16,24},{24,16},{1,9},{9,1},{17,25},{25,17},{2,10},{10... | collective-permute-start | bytes 98312 | tf_op jit(solution)/shard_map/ppermute | solution.py:32
  56.6 5.2 %collective-permute-start.12 = (bf16[64,256]{1,0:T(8,128)(2,1)S(1)}, bf16[64,256]{1,0:T(8,128)(2,1)S(1)}, u32[]{:S(2)}, u32[]{:S(2)}) collective-permute-start(bf16[64,256]{1,0:T(8,128)(2,1)S(1)} %get-tuple-element.42), channel_id=1, source_target_pairs={{8,16},{16,8},{9,17},{17,9},{10,18},{18,10},{11,19},{19,11},{12,20... | collective-permute-start | bytes 98312 | tf_op jit(solution)/shard_map/ppermute | solution.py:33
  61.9 7.1 %collective-permute-start.13 = (bf16[2,68,256]{2,1,0:T(8,128)(2,1)S(1)}, bf16[2,68,256]{2,1,0:T(8,128)(2,1)S(1)}, u32[]{:S(2)}, u32[]{:S(2)}) collective-permute-start(bf16[2,68,256]{2,1,0:T(8,128)(2,1)S(1)} %get-tuple-element.52), channel_id=1, source_target_pairs={{0,1},{1,0},{2,3},{3,2},{4,5},{5,4},{6,7},{7,6},{8,9},{9,8},{10,11... | collective-permute-start | bytes 208904 | tf_op jit(solution)/shard_map/ppermute | solution.py:32
  62.5 6.5 %collective-permute-start.14 = (bf16[2,68,256]{2,1,0:T(8,128)(2,1)S(1)}, bf16[2,68,256]{2,1,0:T(8,128)(2,1)S(1)}, u32[]{:S(2)}, u32[]{:S(2)}) collective-permute-start(bf16[2,68,256]{2,1,0:T(8,128)(2,1)S(1)} %get-tuple-element.51), channel_id=1, source_target_pairs={{1,2},{2,1},{3,4},{4,3},{5,6},{6,5},{9,10},{10,9},{11,12},{12,11},... | collective-permute-start | bytes 208904 | tf_op jit(solution)/shard_map/ppermute | solution.py:33
  (1 other events, 0.9 us)
where the time goes:
time: 72.3 us; the launch traced here: 71.5 us
  Pallas kernels  23.5 us (33%)
  starting transfers between devices  23.2 us (32%)
  waiting for transfers between devices  21.5 us (30%)
  local copies, waits for them, and re-layouts  2.25 us (3%)
  other arithmetic  0.78 us (1%)
    pallas_call x7, Pallas kernels, call(): pl.pallas_call(kernel, out_shape=out_shape, in_specs=[SMEM] * len(scalars...  17.2 us
    ppermute x7, starting transfers between devices, local(): lax.ppermute(outgoing[k], 'gx', [(i, i ^ k) for i in range(peers)])  10.7 us
    ppermute x7, waiting for transfers between devices, local(): lax.ppermute(outgoing[k], 'gx', [(i, i ^ k) for i in range(peers)])  10.7 us
    ppermute x4, waiting for transfers between devices, swap(): first = lax.ppermute(first, axis, near)  10.1 us
    ppermute x4, starting transfers between devices, swap(): second = lax.ppermute(second, axis, far)  8.51 us
    ppermute x4, starting transfers between devices, swap(): first = lax.ppermute(first, axis, near)  3.95 us
    pallas_call x1, Pallas kernels, local(): pl.pallas_call(second_core_kernel, name='second_core', out_shape=(out_sha...  3.84 us
    pallas_call x1, Pallas kernels, local(): pl.pallas_call(edges_kernel, name='edges', out_shape=out_shape, in_specs=...  2.46 us
  transfers between devices with their start and end apart: 15, of which 7 were waited for; matrix products, arithmetic and copies ran while one was open for 0% of the time, Pallas kernels for 20%

commit v1 on v0

--- a/solution.py
+++ b/solution.py
@@ -315,8 +315,6 @@
 WIDE_ROWS = ROWS + 2 * HALO
 MID_ROWS = ROWS + HALO
 RIM_ROWS = 72
-INNER_ROWS = ROWS - 2
-CORE_ROWS = ROWS - 4
 
 
 def tap_columns(weights, dx):
@@ -354,12 +352,13 @@
     return clear(clear(lines, 0), 1)
 
 
-def first_inner_kernel(bev, weights, inner):
-    step = INNER_ROWS // 2
-    for row in range(0, INNER_ROWS, step):
-        block = jnp.maximum(rows_conv(three_rows(bev, row, step), weights), 0.0)
-        block = without_sides(block).reshape(step * COLS, -1).astype(BF16)
-        inner[row * COLS : (row + step) * COLS, :] = block
+EARLY_ROWS = 38
+LATE_ROWS = ROWS - 2 - EARLY_ROWS
+
+
+def first_early_kernel(bev, weights, early):
+    block = jnp.maximum(rows_conv(three_rows(bev, 0, EARLY_ROWS), weights), 0.0)
+    early[...] = without_sides(block).reshape(early.shape).astype(BF16)
 
 
 def strips(upper, lower):
@@ -372,7 +371,7 @@
 
 def second_core_kernel(
     links,
-    inner,
+    early,
     bev,
     first_row,
     second_row,
@@ -380,61 +379,52 @@
     weights_second,
     out,
     flanks,
-    ends,
-    middle,
+    tail,
+    first,
+    head,
     above,
     below,
-    sems,
+    sem,
 ):
     ch = bev.shape[1]
     two = HALO * COLS
-    steps = 2
-    step = CORE_ROWS // steps
-
-    def store(lines, row, keep):
-        count = lines.shape[0]
+    route(links[3, 6], first_row, second_row, below, above)
+    high = jnp.concatenate([above[...], bev[0:two, :]], 0)
+    low = jnp.concatenate([bev[ROWS * COLS - two :, :], below[...]], 0)
+    lhs = jnp.concatenate([strips(high, low), three_rows(bev, EARLY_ROWS, LATE_ROWS)], 0)
+    lines = without_sides(jnp.maximum(rows_conv(lhs, weights_first), 0.0))
+    ends = lines[0 : 2 * HALO]
+    line = lax.broadcasted_iota(jnp.int32, ends.shape, 0)
+    keep = jnp.where(line == 0, links[3, 0], jnp.where(line == 3, links[3, 1], 1)).astype(F32)
+    ends = (ends * keep).reshape(2 * two, ch).astype(BF16)
+    late = lines[2 * HALO :].reshape(LATE_ROWS * COLS, ch).astype(BF16)
+    first[0:two, :] = ends[0:two]
+    first[two : two + EARLY_ROWS * COLS, :] = early[...]
+    first[two + EARLY_ROWS * COLS : ROWS * COLS, :] = late
+    first[ROWS * COLS :, :] = ends[two:]
+
+    step = ROWS // 2
+    copy = pltpu.make_async_copy(head, out.at[0:step], sem)
+    for row, keep in ((0, head), (step, tail)):
+        lines = rows_conv(three_rows(first, row, step), weights_second)
+        own = bev[row * COLS : (row + step) * COLS, :].astype(F32)
+        lines = lines + own.reshape(lines.shape)
         keep[...] = lines.astype(BF16)
         for side, x in enumerate((0, COLS - EDGE)):
-            flank = lines[:, x : x + EDGE, :].reshape(count * EDGE, ch)
+            flank = lines[:, x : x + EDGE, :].reshape(step * EDGE, ch)
             to = (side * ROWS + row) * EDGE
             for h, lanes in halves(ch):
-                flanks[h, to : to + count * EDGE, :] = flank[:, lanes]
-
-    copies = []
-    for k in range(steps):
-        row = k * step + HALO
-        lines = rows_conv(three_rows(inner, k * step, step), weights_second)
-        own = bev[row * COLS : (row + step) * COLS, :].astype(F32)
-        kept = middle.at[k * step : (k + 1) * step]
-        store(lines + own.reshape(lines.shape), row, kept)
-        copies.append(pltpu.make_async_copy(kept, out.at[row : row + step], sems.at[k]))
-        copies[-1].start()
-
-    route(links[3, 6], first_row, second_row, below, above)
-    top, bottom = bev[0:two, :], bev[ROWS * COLS - two :, :]
-    high = jnp.concatenate([above[...], top], 0)
-    low = jnp.concatenate([bottom, below[...]], 0)
-    strip = without_sides(jnp.maximum(rows_conv(strips(high, low), weights_first), 0.0))
-    line = lax.broadcasted_iota(jnp.int32, strip.shape, 0)
-    keep = jnp.where(line == 0, links[3, 0], jnp.where(line == 3, links[3, 1], 1)).astype(F32)
-    strip = (strip * keep).reshape(2 * two, ch).astype(BF16)
-
-    high = jnp.concatenate([strip[0:two], inner[0:two, :]], 0)
-    low = jnp.concatenate([inner[INNER_ROWS * COLS - two :, :], strip[two:]], 0)
-    lines = rows_conv(strips(high, low), weights_second)
-    own = jnp.concatenate([top, bottom], 0).astype(F32)
-    lines = lines + own.reshape(lines.shape)
-    store(lines[0:HALO], 0, ends.at[0:HALO])
-    store(lines[HALO:], ROWS - HALO, ends.at[HALO:])
-    for copy in copies:
-        copy.wait()
+                flanks[h, to : to + step * EDGE, :] = flank[:, lanes]
+        if row == 0:
+            copy.start()
+    copy.wait()
 
 
 def edges_kernel(
     links,
     unused,
     flanks,
-    ends,
+    tail,
     own_left,
     own_right,
     first_in,
@@ -468,12 +458,10 @@
         place(6, second_in)
 
     inner_columns = slice(EDGE, COLS - EDGE)
-    copies = []
-    for k, (row, source) in enumerate(((0, 0), (ROWS - HALO, HALO))):
-        kept = ends.at[source : source + HALO, inner_columns, :]
-        to = out.at[row : row + HALO, inner_columns, :]
-        copies.append(pltpu.make_async_copy(kept, to, sems.at[k]))
-        copies[-1].start()
+    row = ROWS - tail.shape[0]
+    kept = tail.at[:, inner_columns, :]
+    copies = [pltpu.make_async_copy(kept, out.at[row:, inner_columns, :], sems.at[2])]
+    copies[0].start()
     tall = sides.shape[1]
     total[...] = flanks[...]
     narrow = [sides[k, :, :].astype(BF16) for k in range(8)]
@@ -516,7 +504,7 @@
         for h, lanes in halves(ch):
             edge[side, :, :, lanes] = total[h, group, :].reshape(ROWS, EDGE, LANES).astype(BF16)
         copies.append(
-            pltpu.make_async_copy(edge.at[side], out.at[:, x : x + EDGE, :], sems.at[2 + side])
+            pltpu.make_async_copy(edge.at[side], out.at[:, x : x + EDGE, :], sems.at[side])
         )
         copies[-1].start()
     for copy in copies:
@@ -620,13 +608,13 @@
         (pltpu.VMEM((mapped // LANES, ROWS * COLS, LANES), F32), row, row),
     )
     first_row, second_row = swap(first, second, "gy")
-    inner = call(
-        first_inner_kernel,
-        jax.ShapeDtypeStruct((INNER_ROWS * COLS, mapped), BF16),
+    early = call(
+        first_early_kernel,
+        jax.ShapeDtypeStruct((EARLY_ROWS * COLS, mapped), BF16),
         (),
         (bev, k_first),
     )
-    first_row, second_row, inner = lax.optimization_barrier((first_row, second_row, inner))
+    first_row, second_row, early = lax.optimization_barrier((first_row, second_row, early))
     odd_y, odd_x = gy % 2 == 1, gx % 2 == 1
     corner_above = jnp.where(odd_y, first_row, second_row).reshape(HALO, COLS, mapped)
     corner_below = jnp.where(odd_y, second_row, first_row).reshape(HALO, COLS, mapped)
@@ -648,24 +636,26 @@
     flank = (mapped // LANES, 2 * ROWS * EDGE, LANES)
     out_shape = jax.ShapeDtypeStruct((ROWS, COLS, mapped), BF16)
     limit = pltpu.CompilerParams(vmem_limit_bytes=12 << 20)
-    out, flanks, ends = pl.pallas_call(
+    half = (ROWS // 2, COLS, mapped)
+    out, flanks, tail = pl.pallas_call(
         second_core_kernel,
         name="second_core",
         out_shape=(
             out_shape,
             jax.ShapeDtypeStruct(flank, F32),
-            jax.ShapeDtypeStruct((2 * HALO, COLS, mapped), BF16),
+            jax.ShapeDtypeStruct(half, BF16),
         ),
         in_specs=[SMEM] + [VMEM] * 6,
         out_specs=[ANY, VMEM, VMEM],
         scratch_shapes=[
-            pltpu.VMEM((CORE_ROWS, COLS, mapped), BF16),
+            pltpu.VMEM((MID_ROWS * COLS, mapped), BF16),
+            pltpu.VMEM(half, BF16),
             row,
             row,
-            pltpu.SemaphoreType.DMA((2,)),
+            pltpu.SemaphoreType.DMA,
         ],
         compiler_params=limit,
-    )(links, inner, bev, first_row, second_row, k_first, k_second)
+    )(links, early, bev, first_row, second_row, k_first, k_second)
     return pl.pallas_call(
         edges_kernel,
         name="edges",
@@ -676,11 +666,11 @@
             pltpu.VMEM((8, RIM_ROWS + EDGE, mapped), F32),
             pltpu.VMEM(flank, F32),
             pltpu.VMEM((2, ROWS, EDGE, mapped), BF16),
-            pltpu.SemaphoreType.DMA((4,)),
+            pltpu.SemaphoreType.DMA((3,)),
         ],
         input_output_aliases={1: 0},
         compiler_params=limit,
-    )(links, out, flanks, ends, own_left, own_right, first, second, k_first, k_second)
+    )(links, out, flanks, tail, own_left, own_right, first, second, k_first, k_second)
 
 
 def solution(mesh):

time: 72.3 us -> 73.2 us (1.012)
  the two profiles are of different devices: /device:TPU:9 before, /device:TPU:3 now
where the time goes in v1:
time: 73.2 us; the launch traced here: 72.9 us
  starting transfers between devices  30.9 us (42%)
  Pallas kernels  23.5 us (32%)
  waiting for transfers between devices  15.2 us (21%)
  local copies, waits for them, and re-layouts  2.24 us (3%)
  other arithmetic  0.78 us (1%)
    pallas_call x7, Pallas kernels, call(): pl.pallas_call(kernel, out_shape=out_shape, in_specs=[SMEM] * len(scalars...  16.3 us
    ppermute x4, starting transfers between devices, swap(): second = lax.ppermute(second, axis, far)  15.3 us
    ppermute x7, starting transfers between devices, local(): lax.ppermute(outgoing[k], 'gx', [(i, i ^ k) for i in range(peers)])  11.7 us
    ppermute x4, waiting for transfers between devices, swap(): first = lax.ppermute(first, axis, near)  8.72 us
    ppermute x7, waiting for transfers between devices, local(): lax.ppermute(outgoing[k], 'gx', [(i, i ^ k) for i in range(peers)])  5.26 us
    pallas_call x1, Pallas kernels, local(): pl.pallas_call(second_core_kernel, name='second_core', out_shape=(out_sha...  4.79 us
    ppermute x4, starting transfers between devices, swap(): first = lax.ppermute(first, axis, near)  3.89 us
    pallas_call x1, Pallas kernels, local(): pl.pallas_call(edges_kernel, name='edges', out_shape=out_shape, in_specs=...  2.45 us
  transfers between devices with their start and end apart: 15, of which 4 were waited for; matrix products, arithmetic and copies ran while one was open for 0% of the time, Pallas kernels for 19%

profile of v1, /device:TPU:3, one launch (start us, length us, event | category | flops | bytes accessed | tf_op | source)
XLA Modules:
  0.0 72.9 jit_solution(16170624459173855140)
XLA Ops:
  0.7 1.2 %copy-done.1 = bf16[8,512,128]{2,1,0:T(8,128)(2,1)S(1)} copy-done((bf16[8,512,128]{2,1,0:T(8,128)(2,1)S(1)}, bf16[8,512,128]{2,1,0:T(8,128)(2,1)}, u32[]{:S(2)}) %copy-start.1) | copy-done | bytes 1048600
  1.9 0.9 %shard_map.101 = (bf16[1088,128]{1,0:T(8,128)(2,1)S(1)}, bf16[1088,128]{1,0:T(8,128)(2,1)S(1)}) custom-call(s32[4,8]{1,0:T(4,128)S(1)} %pad_add_fusion.links, bf16[4096,128]{1,0:T(8,128)(2,1)S(1)} %bitcast.21), custom_call_target="tpu_custom_call" | custom-call | tf_op jit(solution)/shard_map/pallas_call | solution.py:516
  3.0 4.4 %collective-permute-start.1 = (bf16[1088,128]{1,0:T(8,128)(2,1)S(1)}, bf16[1088,128]{1,0:T(8,128)(2,1)S(1)}, u32[]{:S(2)}, u32[]{:S(2)}) collective-permute-start(bf16[1088,128]{1,0:T(8,128)(2,1)S(1)} %get-tuple-element.29), channel_id=1, source_target_pairs={{1,2},{2,1},{3,4},{4,3},{5,6},{6,5},{7,8},{8,7},{9,10},{10,9},{11,... | collective-permute-start | bytes 835592 | tf_op jit(solution)/shard_map/ppermute | solution.py:33
  8.3 3.8 %shard_map.100.partial = f32[4096,128]{1,0:T(8,128)S(1)} custom-call(s32[4,8]{1,0:T(4,128)S(1)} %pad_add_fusion.links, bf16[4096,128]{1,0:T(8,128)(2,1)S(1)} %bitcast.22, bf16[896,128]{1,0:T(8,128)(2,1)S(1)} %bitcast.26), custom_call_target="tpu_custom_call" | custom-call | tf_op jit(solution)/shard_map/pallas_call | solution.py:516
  12.1 4.3 %collective-permute-done.first_in = bf16[1088,128]{1,0:T(8,128)(2,1)S(1)} collective-permute-done((bf16[1088,128]{1,0:T(8,128)(2,1)S(1)}, bf16[1088,128]{1,0:T(8,128)(2,1)S(1)}, u32[]{:S(2)}, u32[]{:S(2)}) %collective-permute-start) | collective-permute-done | bytes 278560 | tf_op jit(solution)/shard_map/ppermute | solution.py:32
  16.5 1.4 %shard_map.102 = (bf16[4096,128]{1,0:T(8,128)(2,1)S(1)}, bf16[1088,128]{1,0:T(8,128)(2,1)S(1)}, bf16[1088,128]{1,0:T(8,128)(2,1)S(1)}) custom-call(s32[4,8]{1,0:T(4,128)S(1)} %pad_add_fusion.links, f32[4096,128]{1,0:T(8,128)S(1)} %shard_map.100.partial, bf16[1088,128]{1,0:T(8,128)(2,1)S(1)} %collective-permute-done.first_in, ...), custom_call_target="tpu_custom_call" | custom-call | tf_op jit(solution)/shard_map/pallas_call | solution.py:516
  18.2 4.1 %collective-permute-start.3 = (bf16[1088,128]{1,0:T(8,128)(2,1)S(1)}, bf16[1088,128]{1,0:T(8,128)(2,1)S(1)}, u32[]{:S(2)}, u32[]{:S(2)}) collective-permute-start(bf16[1088,128]{1,0:T(8,128)(2,1)S(1)} %get-tuple-element.32), channel_id=1, source_target_pairs={{1,2},{2,1},{3,4},{4,3},{5,6},{6,5},{7,8},{8,7},{9,10},{10,9},{11,... | collective-permute-start | bytes 835592 | tf_op jit(solution)/shard_map/ppermute | solution.py:33
  22.4 3.8 %shard_map.103.partial = f32[4096,128]{1,0:T(8,128)S(1)} custom-call(s32[4,8]{1,0:T(4,128)S(1)} %pad_add_fusion.links, bf16[4096,128]{1,0:T(8,128)(2,1)S(1)} %get-tuple-element.30.hidden, bf16[4096,128]{1,0:T(8,128)(2,1)S(1)} %bitcast.23, bf16[896,128]{1,0:T(8,128)(2,1)S(1)} %bitcast.28), custom_call_target="tpu_custom_call" | custom-call | tf_op jit(solution)/shard_map/pallas_call | solution.py:516
  26.2 4.4 %collective-permute-done.2.first_in = bf16[1088,128]{1,0:T(8,128)(2,1)S(1)} collective-permute-done((bf16[1088,128]{1,0:T(8,128)(2,1)S(1)}, bf16[1088,128]{1,0:T(8,128)(2,1)S(1)}, u32[]{:S(2)}, u32[]{:S(2)}) %collective-permute-start.2) | collective-permute-done | bytes 278560 | tf_op jit(solution)/shard_map/ppermute | solution.py:32
  30.7 3.3 %shard_map.104 = (bf16[264,128]{1,0:T(8,128)(2,1)S(1)}, bf16[264,128]{1,0:T(8,128)(2,1)S(1)}, bf16[264,128]{1,0:T(8,128)(2,1)S(1)}, bf16[264,128]{1,0:T(8,128)(2...) custom-call(s32[4,8]{1,0:T(4,128)S(1)} %pad_add_fusion.links, ...), custom_call_target="tpu_custom_call" | custom-call | tf_op jit(solution)/shard_map/pallas_call | solution.py:516
  34.0 1.5 %collective-permute-start.4 = (bf16[264,128]{1,0:T(8,128)(2,1)S(1)}, bf16[264,128]{1,0:T(8,128)(2,1)S(1)}, u32[]{:S(2)}, u32[]{:S(2)}) collective-permute-start(bf16[264,128]{1,0:T(8,128)(2,1)S(1)} %get-tuple-element.34), channel_id=1, source_target_pairs={{0,1},{1,0},{2,3},{3,2},{4,5},{5,4},{6,7},{7,6},{8,9},{9,8},{10,11... | collective-permute-start | bytes 202760 | tf_op jit(solution)/shard_map/ppermute | solution.py:594
  35.5 1.3 %collective-permute-start.6 = (bf16[264,128]{1,0:T(8,128)(2,1)S(1)}, bf16[264,128]{1,0:T(8,128)(2,1)S(1)}, u32[]{:S(2)}, u32[]{:S(2)}) collective-permute-start(bf16[264,128]{1,0:T(8,128)(2,1)S(1)} %get-tuple-element.36), channel_id=1, source_target_pairs={{0,3},{1,2},{2,1},{3,0},{4,7},{5,6},{6,5},{7,4},{8,11},{9,10},{10,... | collective-permute-start | bytes 202760 | tf_op jit(solution)/shard_map/ppermute | solution.py:594
  36.7 4.4 %collective-permute-start.7 = (bf16[264,128]{1,0:T(8,128)(2,1)S(1)}, bf16[264,128]{1,0:T(8,128)(2,1)S(1)}, u32[]{:S(2)}, u32[]{:S(2)}) collective-permute-start(bf16[264,128]{1,0:T(8,128)(2,1)S(1)} %get-tuple-element.37), channel_id=1, source_target_pairs={{0,4},{1,5},{2,6},{3,7},{4,0},{5,1},{6,2},{7,3},{8,12},{9,13},{10,... | collective-permute-start | bytes 202760 | tf_op jit(solution)/shard_map/ppermute | solution.py:594
  41.2 3.3 %collective-permute-start.9 = (bf16[264,128]{1,0:T(8,128)(2,1)S(1)}, bf16[264,128]{1,0:T(8,128)(2,1)S(1)}, u32[]{:S(2)}, u32[]{:S(2)}) collective-permute-start(bf16[264,128]{1,0:T(8,128)(2,1)S(1)} %get-tuple-element.39), channel_id=1, source_target_pairs={{0,6},{1,7},{2,4},{3,5},{4,2},{5,3},{6,0},{7,1},{8,14},{9,15},{10,... | collective-permute-start | bytes 202760 | tf_op jit(solution)/shard_map/ppermute | solution.py:594
  44.5 1.2 %collective-permute-start.10 = (bf16[264,128]{1,0:T(8,128)(2,1)S(1)}, bf16[264,128]{1,0:T(8,128)(2,1)S(1)}, u32[]{:S(2)}, u32[]{:S(2)}) collective-permute-start(bf16[264,128]{1,0:T(8,128)(2,1)S(1)} %get-tuple-element.40), channel_id=1, source_target_pairs={{0,7},{1,6},{2,5},{3,4},{4,3},{5,2},{6,1},{7,0},{8,15},{9,14},{10,... | collective-permute-start | bytes 202760 | tf_op jit(solution)/shard_map/ppermute | solution.py:594
  45.7 5.2 %collective-permute-done.8.refs_5_ = bf16[264,128]{1,0:T(8,128)(2,1)S(1)} collective-permute-done((bf16[264,128]{1,0:T(8,128)(2,1)S(1)}, bf16[264,128]{1,0:T(8,128)(2,1)S(1)}, u32[]{:S(2)}, u32[]{:S(2)}) %collective-permute-start.8) | collective-permute-done | bytes 67616 | tf_op jit(solution)/shard_map/ppermute | solution.py:594
  51.0 1.3 %shard_map.105 = (bf16[2048,256]{1,0:T(8,128)(2,1)S(1)}, bf16[64,256]{1,0:T(8,128)(2,1)S(1)}, bf16[64,256]{1,0:T(8,128)(2,1)S(1)}, bf16[4,64,256]{2,1,0:T(8,128)(2,1)S(1)}) custom-call(s32[4,8]{1,0:T(4,128)S(1)} %pad_add_fusion.links, bf16[264,128]{1,0:T(8,128)(2,1)S(1)} %get-tuple-element.33.refs_0_, bf16[264,128]{1,0:T(8,128)(2,1)S(1)} %collective-permute-done.4.refs_1_, ...), custom_call_target="tpu_custom_call" | custom-call | tf_op jit(solution)/shard_map/pallas_call | solution.py:516
  52.2 3.4 %collective-permute-start.11 = (bf16[64,256]{1,0:T(8,128)(2,1)S(1)}, bf16[64,256]{1,0:T(8,128)(2,1)S(1)}, u32[]{:S(2)}, u32[]{:S(2)}) collective-permute-start(bf16[64,256]{1,0:T(8,128)(2,1)S(1)} %get-tuple-element.41), channel_id=1, source_target_pairs={{0,8},{8,0},{16,24},{24,16},{1,9},{9,1},{17,25},{25,17},{2,10},{10... | collective-permute-start | bytes 98312 | tf_op jit(solution)/shard_map/ppermute | solution.py:32
  55.6 2.3 %collective-permute-start.12 = (bf16[64,256]{1,0:T(8,128)(2,1)S(1)}, bf16[64,256]{1,0:T(8,128)(2,1)S(1)}, u32[]{:S(2)}, u32[]{:S(2)}) collective-permute-start(bf16[64,256]{1,0:T(8,128)(2,1)S(1)} %get-tuple-element.42), channel_id=1, source_target_pairs={{8,16},{16,8},{9,17},{17,9},{10,18},{18,10},{11,19},{19,11},{12,20... | collective-permute-start | bytes 98312 | tf_op jit(solution)/shard_map/ppermute | solution.py:33
  58.0 1.7 %shard_map.106.early = bf16[1216,256]{1,0:T(8,128)(2,1)S(1)} custom-call(bf16[2048,256]{1,0:T(8,128)(2,1)S(1)} %get-tuple-element.43.bev, bf16[9,256,256]{2,1,0:T(8,128)(2,1)S(1)} %bitcast.18), custom_call_target="tpu_custom_call" | custom-call | tf_op jit(solution)/shard_map/pallas_call | solution.py:516
  59.7 1.2 %collective-permute-done.12.second_row = bf16[64,256]{1,0:T(8,128)(2,1)S(1)} collective-permute-done((bf16[64,256]{1,0:T(8,128)(2,1)S(1)}, bf16[64,256]{1,0:T(8,128)(2,1)S(1)}, u32[]{:S(2)}, u32[]{:S(2)}) %collective-permute-start.12) | collective-permute-done | bytes 32800 | tf_op jit(solution)/shard_map/ppermute | solution.py:33
  61.1 4.5 %collective-permute-start.14 = (bf16[2,68,256]{2,1,0:T(8,128)(2,1)S(1)}, bf16[2,68,256]{2,1,0:T(8,128)(2,1)S(1)}, u32[]{:S(2)}, u32[]{:S(2)}) collective-permute-start(bf16[2,68,256]{2,1,0:T(8,128)(2,1)S(1)} %get-tuple-element.51), channel_id=1, source_target_pairs={{1,2},{2,1},{3,4},{4,3},{5,6},{6,5},{9,10},{10,9},{11,12},{12,11},... | collective-permute-start | bytes 208904 | tf_op jit(solution)/shard_map/ppermute | solution.py:33
  65.6 4.8 %second_core.1 = (bf16[64,32,256]{2,1,0:T(8,128)(2,1)}, f32[2,1024,128]{2,1,0:T(8,128)S(1)}, bf16[32,32,256]{2,1,0:T(8,128)(2,1)S(1)}) custom-call(s32[4,8]{1,0:T(4,128)S(1)} %pad_add_fusion.links, bf16[1216,256]{1,0:T(8,128)(2,1)S(1)} %shard_map.106.early, bf16[2048,256]{1,0:T(8,128)(2,1)S(1)} %get-tuple-element.43.bev, ...), custom_call_target="tpu_custom_call" | custom-call | tf_op jit(solution)/shard_map/second_core/pallas_call | solution.py:640
  70.5 2.5 %edges.1 = bf16[64,32,256]{2,1,0:T(8,128)(2,1)} custom-call(s32[4,8]{1,0:T(4,128)S(1)} %pad_add_fusion.links, bf16[64,32,256]{2,1,0:T(8,128)(2,1)} %get-tuple-element.47.unused, f32[2,1024,128]{2,1,0:T(8,128)S(1)} %get-tuple-element.48.flanks, bf16[32,32,256]{2,1,0:T(8,128)(2,1)S(1)} %get-tuple-element.49.tail, ...), custom_call_target="tpu_custom_call", output_to_operand_aliasing={{}: (1, {})} | custom-call | tf_op jit(solution)/shard_map/edges/pallas_call | solution.py:659
  (44 shorter events, 2.3 us)
Async XLA Ops:
  0.7 1.2 %copy-start.1 = (bf16[8,512,128]{2,1,0:T(8,128)(2,1)S(1)}, bf16[8,512,128]{2,1,0:T(8,128)(2,1)}, u32[]{:S(2)}) copy-start(bf16[8,512,128]{2,1,0:T(8,128)(2,1)} %param.10) | copy-start | bytes 3145732
  2.9 13.6 %collective-permute-start = (bf16[1088,128]{1,0:T(8,128)(2,1)S(1)}, bf16[1088,128]{1,0:T(8,128)(2,1)S(1)}, u32[]{:S(2)}, u32[]{:S(2)}) collective-permute-start(bf16[1088,128]{1,0:T(8,128)(2,1)S(1)} %get-tuple-element.28), channel_id=1, source_target_pairs={{0,1},{1,0},{2,3},{3,2},{4,5},{5,4},{6,7},{7,6},{8,9},{9,8},{10,11... | collective-permute-start | bytes 835592 | tf_op jit(solution)/shard_map/ppermute | solution.py:32
  3.0 13.5 %collective-permute-start.1 = (bf16[1088,128]{1,0:T(8,128)(2,1)S(1)}, bf16[1088,128]{1,0:T(8,128)(2,1)S(1)}, u32[]{:S(2)}, u32[]{:S(2)}) collective-permute-start(bf16[1088,128]{1,0:T(8,128)(2,1)S(1)} %get-tuple-element.29), channel_id=1, source_target_pairs={{1,2},{2,1},{3,4},{4,3},{5,6},{6,5},{7,8},{8,7},{9,10},{10,9},{11,... | collective-permute-start | bytes 835592 | tf_op jit(solution)/shard_map/ppermute | solution.py:33
  12.1 10.3 %copy-start.2 = (bf16[8,512,128]{2,1,0:T(8,128)(2,1)S(1)}, bf16[8,512,128]{2,1,0:T(8,128)(2,1)}, u32[]{:S(2)}) copy-start(bf16[8,512,128]{2,1,0:T(8,128)(2,1)} %param.10) | copy-start | bytes 3145732
  12.1 10.3 %copy-start.6 = (bf16[7,128,128]{2,1,0:T(8,128)(2,1)S(1)}, bf16[7,128,128]{2,1,0:T(8,128)(2,1)}, u32[]{:S(2)}) copy-start(bf16[7,128,128]{2,1,0:T(8,128)(2,1)} %param.16) | copy-start | bytes 688132
  17.9 12.7 %collective-permute-start.2 = (bf16[1088,128]{1,0:T(8,128)(2,1)S(1)}, bf16[1088,128]{1,0:T(8,128)(2,1)S(1)}, u32[]{:S(2)}, u32[]{:S(2)}) collective-permute-start(bf16[1088,128]{1,0:T(8,128)(2,1)S(1)} %get-tuple-element.31), channel_id=1, source_target_pairs={{0,1},{1,0},{2,3},{3,2},{4,5},{5,4},{6,7},{7,6},{8,9},{9,8},{10,11... | collective-permute-start | bytes 835592 | tf_op jit(solution)/shard_map/ppermute | solution.py:32
  18.2 12.4 %collective-permute-start.3 = (bf16[1088,128]{1,0:T(8,128)(2,1)S(1)}, bf16[1088,128]{1,0:T(8,128)(2,1)S(1)}, u32[]{:S(2)}, u32[]{:S(2)}) collective-permute-start(bf16[1088,128]{1,0:T(8,128)(2,1)S(1)} %get-tuple-element.32), channel_id=1, source_target_pairs={{1,2},{2,1},{3,4},{4,3},{5,6},{6,5},{7,8},{8,7},{9,10},{10,9},{11,... | collective-permute-start | bytes 835592 | tf_op jit(solution)/shard_map/ppermute | solution.py:33
  22.4 8.3 %copy-start.4 = (bf16[4,1024,256]{2,1,0:T(8,128)(2,1)S(1)}, bf16[4,1024,256]{2,1,0:T(8,128)(2,1)}, u32[]{:S(2)}) copy-start(bf16[4,1024,256]{2,1,0:T(8,128)(2,1)} %height.1) | copy-start | bytes 6291460
  22.4 8.2 %copy-start.7 = (s32[8]{0:T(128)S(1)}, s32[8]{0:T(128)}, u32[]{:S(2)}) copy-start(s32[8]{0:T(128)} %param.12) | copy-start | bytes 100
  22.4 8.2 %copy-start.8 = (s32[8]{0:T(128)S(1)}, s32[8]{0:T(128)}, u32[]{:S(2)}) copy-start(s32[8]{0:T(128)} %param.13) | copy-start | bytes 100
  22.4 8.2 %copy-start.9 = (s32[1,16]{1,0:T(1,128)S(1)}, s32[1,16]{1,0:T(1,128)}, u32[]{:S(2)}) copy-start(s32[1,16]{1,0:T(1,128)} %columns.1) | copy-start | bytes 196
  30.7 27.3 %copy-start = (bf16[3,3,256,256]{3,2,1,0:T(8,128)(2,1)S(1)}, bf16[3,3,256,256]{3,2,1,0:T(8,128)(2,1)}, u32[]{:S(2)}) copy-start(bf16[3,3,256,256]{3,2,1,0:T(8,128)(2,1)} %param.18) | copy-start | bytes 3538948
  34.0 7.2 %collective-permute-start.4 = (bf16[264,128]{1,0:T(8,128)(2,1)S(1)}, bf16[264,128]{1,0:T(8,128)(2,1)S(1)}, u32[]{:S(2)}, u32[]{:S(2)}) collective-permute-start(bf16[264,128]{1,0:T(8,128)(2,1)S(1)} %get-tuple-element.34), channel_id=1, source_target_pairs={{0,1},{1,0},{2,3},{3,2},{4,5},{5,4},{6,7},{7,6},{8,9},{9,8},{10,11... | collective-permute-start | bytes 202760 | tf_op jit(solution)/shard_map/ppermute | solution.py:594
  35.5 9.0 %collective-permute-start.5 = (bf16[264,128]{1,0:T(8,128)(2,1)S(1)}, bf16[264,128]{1,0:T(8,128)(2,1)S(1)}, u32[]{:S(2)}, u32[]{:S(2)}) collective-permute-start(bf16[264,128]{1,0:T(8,128)(2,1)S(1)} %get-tuple-element.35), channel_id=1, source_target_pairs={{0,2},{1,3},{2,0},{3,1},{4,6},{5,7},{6,4},{7,5},{8,10},{9,11},{10,... | collective-permute-start | bytes 202760 | tf_op jit(solution)/shard_map/ppermute | solution.py:594
  35.5 10.2 %collective-permute-start.6 = (bf16[264,128]{1,0:T(8,128)(2,1)S(1)}, bf16[264,128]{1,0:T(8,128)(2,1)S(1)}, u32[]{:S(2)}, u32[]{:S(2)}) collective-permute-start(bf16[264,128]{1,0:T(8,128)(2,1)S(1)} %get-tuple-element.36), channel_id=1, source_target_pairs={{0,3},{1,2},{2,1},{3,0},{4,7},{5,6},{6,5},{7,4},{8,11},{9,10},{10,... | collective-permute-start | bytes 202760 | tf_op jit(solution)/shard_map/ppermute | solution.py:594
  36.7 9.0 %collective-permute-start.7 = (bf16[264,128]{1,0:T(8,128)(2,1)S(1)}, bf16[264,128]{1,0:T(8,128)(2,1)S(1)}, u32[]{:S(2)}, u32[]{:S(2)}) collective-permute-start(bf16[264,128]{1,0:T(8,128)(2,1)S(1)} %get-tuple-element.37), channel_id=1, source_target_pairs={{0,4},{1,5},{2,6},{3,7},{4,0},{5,1},{6,2},{7,3},{8,12},{9,13},{10,... | collective-permute-start | bytes 202760 | tf_op jit(solution)/shard_map/ppermute | solution.py:594
  41.2 9.8 %collective-permute-start.8 = (bf16[264,128]{1,0:T(8,128)(2,1)S(1)}, bf16[264,128]{1,0:T(8,128)(2,1)S(1)}, u32[]{:S(2)}, u32[]{:S(2)}) collective-permute-start(bf16[264,128]{1,0:T(8,128)(2,1)S(1)} %get-tuple-element.38), channel_id=1, source_target_pairs={{0,5},{1,4},{2,7},{3,6},{4,1},{5,0},{6,3},{7,2},{8,13},{9,12},{10,... | collective-permute-start | bytes 202760 | tf_op jit(solution)/shard_map/ppermute | solution.py:594
  41.2 9.8 %collective-permute-start.9 = (bf16[264,128]{1,0:T(8,128)(2,1)S(1)}, bf16[264,128]{1,0:T(8,128)(2,1)S(1)}, u32[]{:S(2)}, u32[]{:S(2)}) collective-permute-start(bf16[264,128]{1,0:T(8,128)(2,1)S(1)} %get-tuple-element.39), channel_id=1, source_target_pairs={{0,6},{1,7},{2,4},{3,5},{4,2},{5,3},{6,0},{7,1},{8,14},{9,15},{10,... | collective-permute-start | bytes 202760 | tf_op jit(solution)/shard_map/ppermute | solution.py:594
  44.5 6.4 %collective-permute-start.10 = (bf16[264,128]{1,0:T(8,128)(2,1)S(1)}, bf16[264,128]{1,0:T(8,128)(2,1)S(1)}, u32[]{:S(2)}, u32[]{:S(2)}) collective-permute-start(bf16[264,128]{1,0:T(8,128)(2,1)S(1)} %get-tuple-element.40), channel_id=1, source_target_pairs={{0,7},{1,6},{2,5},{3,4},{4,3},{5,2},{6,1},{7,0},{8,15},{9,14},{10,... | collective-permute-start | bytes 202760 | tf_op jit(solution)/shard_map/ppermute | solution.py:594
  51.0 14.7 %copy-start.3 = (bf16[3,3,256,256]{3,2,1,0:T(8,128)(2,1)S(1)}, bf16[3,3,256,256]{3,2,1,0:T(8,128)(2,1)}, u32[]{:S(2)}) copy-start(bf16[3,3,256,256]{3,2,1,0:T(8,128)(2,1)} %param.19) | copy-start | bytes 3538948
  52.2 7.4 %collective-permute-start.11 = (bf16[64,256]{1,0:T(8,128)(2,1)S(1)}, bf16[64,256]{1,0:T(8,128)(2,1)S(1)}, u32[]{:S(2)}, u32[]{:S(2)}) collective-permute-start(bf16[64,256]{1,0:T(8,128)(2,1)S(1)} %get-tuple-element.41), channel_id=1, source_target_pairs={{0,8},{8,0},{16,24},{24,16},{1,9},{9,1},{17,25},{25,17},{2,10},{10... | collective-permute-start | bytes 98312 | tf_op jit(solution)/shard_map/ppermute | solution.py:32
  55.6 5.2 %collective-permute-start.12 = (bf16[64,256]{1,0:T(8,128)(2,1)S(1)}, bf16[64,256]{1,0:T(8,128)(2,1)S(1)}, u32[]{:S(2)}, u32[]{:S(2)}) collective-permute-start(bf16[64,256]{1,0:T(8,128)(2,1)S(1)} %get-tuple-element.42), channel_id=1, source_target_pairs={{8,16},{16,8},{9,17},{17,9},{10,18},{18,10},{11,19},{19,11},{12,20... | collective-permute-start | bytes 98312 | tf_op jit(solution)/shard_map/ppermute | solution.py:33
  61.0 9.5 %collective-permute-start.13 = (bf16[2,68,256]{2,1,0:T(8,128)(2,1)S(1)}, bf16[2,68,256]{2,1,0:T(8,128)(2,1)S(1)}, u32[]{:S(2)}, u32[]{:S(2)}) collective-permute-start(bf16[2,68,256]{2,1,0:T(8,128)(2,1)S(1)} %get-tuple-element.52), channel_id=1, source_target_pairs={{0,1},{1,0},{2,3},{3,2},{4,5},{5,4},{6,7},{7,6},{8,9},{9,8},{10,11... | collective-permute-start | bytes 208904 | tf_op jit(solution)/shard_map/ppermute | solution.py:32
  61.1 9.4 %collective-permute-start.14 = (bf16[2,68,256]{2,1,0:T(8,128)(2,1)S(1)}, bf16[2,68,256]{2,1,0:T(8,128)(2,1)S(1)}, u32[]{:S(2)}, u32[]{:S(2)}) collective-permute-start(bf16[2,68,256]{2,1,0:T(8,128)(2,1)S(1)} %get-tuple-element.51), channel_id=1, source_target_pairs={{1,2},{2,1},{3,4},{4,3},{5,6},{6,5},{9,10},{10,9},{11,12},{12,11},... | collective-permute-start | bytes 208904 | tf_op jit(solution)/shard_map/ppermute | solution.py:33
  (1 other events, 0.9 us)

commit v2 on v0

--- a/solution.py
+++ b/solution.py
@@ -259,12 +259,9 @@
             rows_in[own, c * ch : (c + 1) * ch] = jnp.maximum(line, 0.0).astype(BF16)
     sums[...] = jnp.zeros_like(sums)
 
-    def one(j, carry):
-        rows = rows_in[pl.ds(pl.multiple_of(j * FACE, FACE), FACE), :]
+    for j in range(count):
+        rows = rows_in[j * FACE : (j + 1) * FACE, :]
         sums[slots[0, j]] += mm(rows, height[block_levels[0, j]])
-        return carry
-
-    lax.fori_loop(0, count, one, 0)
     peers = len(outs)
     per_peer = sums.shape[0] // peers
     row_at = lax.broadcasted_iota(jnp.int32, (ID_ROWS, LANES), 0)

time: 72.3 us -> 71.3 us (0.986)
  Pallas kernels: 23.5 us -> 22.5 us
    pallas_call x7, Pallas kernels: 17.2 us -> 16.2 us  [call(): pl.pallas_call(kernel, out_shape=out_shape, in_specs=[SMEM] * len(scalars...]
where the time goes in v2:
time: 71.3 us; the launch traced here: 70.5 us
  starting transfers between devices  23.2 us (33%)
  Pallas kernels  22.5 us (32%)
  waiting for transfers between devices  21.5 us (30%)
  local copies, waits for them, and re-layouts  2.25 us (3%)
  other arithmetic  0.78 us (1%)
    pallas_call x7, Pallas kernels, call(): pl.pallas_call(kernel, out_shape=out_shape, in_specs=[SMEM] * len(scalars...  16.2 us
    ppermute x7, starting transfers between devices, local(): lax.ppermute(outgoing[k], 'gx', [(i, i ^ k) for i in range(peers)])  10.7 us
    ppermute x7, waiting for transfers between devices, local(): lax.ppermute(outgoing[k], 'gx', [(i, i ^ k) for i in range(peers)])  10.7 us
    ppermute x4, waiting for transfers between devices, swap(): first = lax.ppermute(first, axis, near)  10.1 us
    ppermute x4, starting transfers between devices, swap(): second = lax.ppermute(second, axis, far)  8.51 us
    ppermute x4, starting transfers between devices, swap(): first = lax.ppermute(first, axis, near)  3.95 us
    pallas_call x1, Pallas kernels, local(): pl.pallas_call(second_core_kernel, name='second_core', out_shape=(out_sha...  3.84 us
    pallas_call x1, Pallas kernels, local(): pl.pallas_call(edges_kernel, name='edges', out_shape=out_shape, in_specs=...  2.46 us
  transfers between devices with their start and end apart: 15, of which 7 were waited for; matrix products, arithmetic and copies ran while one was open for 0% of the time, Pallas kernels for 20%

profile of v2, /device:TPU:9, one launch (start us, length us, event | category | flops | bytes accessed | tf_op | source)
XLA Modules:
  0.0 70.5 jit_solution(12803326543623420788)
XLA Ops:
  0.7 1.2 %copy-done.1 = bf16[8,512,128]{2,1,0:T(8,128)(2,1)S(1)} copy-done((bf16[8,512,128]{2,1,0:T(8,128)(2,1)S(1)}, bf16[8,512,128]{2,1,0:T(8,128)(2,1)}, u32[]{:S(2)}) %copy-start.1) | copy-done | bytes 1048600
  2.9 1.3 %collective-permute-start = (bf16[1088,128]{1,0:T(8,128)(2,1)S(1)}, bf16[1088,128]{1,0:T(8,128)(2,1)S(1)}, u32[]{:S(2)}, u32[]{:S(2)}) collective-permute-start(bf16[1088,128]{1,0:T(8,128)(2,1)S(1)} %get-tuple-element.28), channel_id=1, source_target_pairs={{0,1},{1,0},{2,3},{3,2},{4,5},{5,4},{6,7},{7,6},{8,9},{9,8},{10,11... | collective-permute-start | bytes 835592 | tf_op jit(solution)/shard_map/ppermute | solution.py:32
  4.2 1.9 %collective-permute-start.1 = (bf16[1088,128]{1,0:T(8,128)(2,1)S(1)}, bf16[1088,128]{1,0:T(8,128)(2,1)S(1)}, u32[]{:S(2)}, u32[]{:S(2)}) collective-permute-start(bf16[1088,128]{1,0:T(8,128)(2,1)S(1)} %get-tuple-element.29), channel_id=1, source_target_pairs={{1,2},{2,1},{3,4},{4,3},{5,6},{6,5},{7,8},{8,7},{9,10},{10,9},{11,... | collective-permute-start | bytes 835592 | tf_op jit(solution)/shard_map/ppermute | solution.py:33
  7.0 3.8 %shard_map.100.partial = f32[4096,128]{1,0:T(8,128)S(1)} custom-call(s32[4,8]{1,0:T(4,128)S(1)} %pad_add_fusion.links, bf16[4096,128]{1,0:T(8,128)(2,1)S(1)} %bitcast.22, bf16[896,128]{1,0:T(8,128)(2,1)S(1)} %bitcast.26), custom_call_target="tpu_custom_call" | custom-call | tf_op jit(solution)/shard_map/pallas_call | solution.py:525
  10.8 5.6 %collective-permute-done.first_in = bf16[1088,128]{1,0:T(8,128)(2,1)S(1)} collective-permute-done((bf16[1088,128]{1,0:T(8,128)(2,1)S(1)}, bf16[1088,128]{1,0:T(8,128)(2,1)S(1)}, u32[]{:S(2)}, u32[]{:S(2)}) %collective-permute-start) | collective-permute-done | bytes 278560 | tf_op jit(solution)/shard_map/ppermute | solution.py:32
  16.5 1.4 %shard_map.102 = (bf16[4096,128]{1,0:T(8,128)(2,1)S(1)}, bf16[1088,128]{1,0:T(8,128)(2,1)S(1)}, bf16[1088,128]{1,0:T(8,128)(2,1)S(1)}) custom-call(s32[4,8]{1,0:T(4,128)S(1)} %pad_add_fusion.links, f32[4096,128]{1,0:T(8,128)S(1)} %shard_map.100.partial, bf16[1088,128]{1,0:T(8,128)(2,1)S(1)} %collective-permute-done.first_in, ...), custom_call_target="tpu_custom_call" | custom-call | tf_op jit(solution)/shard_map/pallas_call | solution.py:525
  17.9 1.3 %collective-permute-start.2 = (bf16[1088,128]{1,0:T(8,128)(2,1)S(1)}, bf16[1088,128]{1,0:T(8,128)(2,1)S(1)}, u32[]{:S(2)}, u32[]{:S(2)}) collective-permute-start(bf16[1088,128]{1,0:T(8,128)(2,1)S(1)} %get-tuple-element.31), channel_id=1, source_target_pairs={{0,1},{1,0},{2,3},{3,2},{4,5},{5,4},{6,7},{7,6},{8,9},{9,8},{10,11... | collective-permute-start | bytes 835592 | tf_op jit(solution)/shard_map/ppermute | solution.py:32
  19.2 2.0 %collective-permute-start.3 = (bf16[1088,128]{1,0:T(8,128)(2,1)S(1)}, bf16[1088,128]{1,0:T(8,128)(2,1)S(1)}, u32[]{:S(2)}, u32[]{:S(2)}) collective-permute-start(bf16[1088,128]{1,0:T(8,128)(2,1)S(1)} %get-tuple-element.32), channel_id=1, source_target_pairs={{1,2},{2,1},{3,4},{4,3},{5,6},{6,5},{7,8},{8,7},{9,10},{10,9},{11,... | collective-permute-start | bytes 835592 | tf_op jit(solution)/shard_map/ppermute | solution.py:33
  21.3 3.8 %shard_map.103.partial = f32[4096,128]{1,0:T(8,128)S(1)} custom-call(s32[4,8]{1,0:T(4,128)S(1)} %pad_add_fusion.links, bf16[4096,128]{1,0:T(8,128)(2,1)S(1)} %get-tuple-element.30.hidden, bf16[4096,128]{1,0:T(8,128)(2,1)S(1)} %bitcast.23, bf16[896,128]{1,0:T(8,128)(2,1)S(1)} %bitcast.28), custom_call_target="tpu_custom_call" | custom-call | tf_op jit(solution)/shard_map/pallas_call | solution.py:525
  25.1 4.5 %collective-permute-done.2.first_in = bf16[1088,128]{1,0:T(8,128)(2,1)S(1)} collective-permute-done((bf16[1088,128]{1,0:T(8,128)(2,1)S(1)}, bf16[1088,128]{1,0:T(8,128)(2,1)S(1)}, u32[]{:S(2)}, u32[]{:S(2)}) %collective-permute-start.2) | collective-permute-done | bytes 278560 | tf_op jit(solution)/shard_map/ppermute | solution.py:32
  29.7 2.4 %shard_map.104 = (bf16[264,128]{1,0:T(8,128)(2,1)S(1)}, bf16[264,128]{1,0:T(8,128)(2,1)S(1)}, bf16[264,128]{1,0:T(8,128)(2,1)S(1)}, bf16[264,128]{1,0:T(8,128)(2...) custom-call(s32[4,8]{1,0:T(4,128)S(1)} %pad_add_fusion.links, ...), custom_call_target="tpu_custom_call" | custom-call | tf_op jit(solution)/shard_map/pallas_call | solution.py:525
  32.0 2.3 %collective-permute-start.4 = (bf16[264,128]{1,0:T(8,128)(2,1)S(1)}, bf16[264,128]{1,0:T(8,128)(2,1)S(1)}, u32[]{:S(2)}, u32[]{:S(2)}) collective-permute-start(bf16[264,128]{1,0:T(8,128)(2,1)S(1)} %get-tuple-element.34), channel_id=1, source_target_pairs={{0,1},{1,0},{2,3},{3,2},{4,5},{5,4},{6,7},{7,6},{8,9},{9,8},{10,11... | collective-permute-start | bytes 202760 | tf_op jit(solution)/shard_map/ppermute | solution.py:603
  35.6 4.6 %collective-permute-start.7 = (bf16[264,128]{1,0:T(8,128)(2,1)S(1)}, bf16[264,128]{1,0:T(8,128)(2,1)S(1)}, u32[]{:S(2)}, u32[]{:S(2)}) collective-permute-start(bf16[264,128]{1,0:T(8,128)(2,1)S(1)} %get-tuple-element.37), channel_id=1, source_target_pairs={{0,4},{1,5},{2,6},{3,7},{4,0},{5,1},{6,2},{7,3},{8,12},{9,13},{10,... | collective-permute-start | bytes 202760 | tf_op jit(solution)/shard_map/ppermute | solution.py:603
  41.3 1.2 %collective-permute-start.9 = (bf16[264,128]{1,0:T(8,128)(2,1)S(1)}, bf16[264,128]{1,0:T(8,128)(2,1)S(1)}, u32[]{:S(2)}, u32[]{:S(2)}) collective-permute-start(bf16[264,128]{1,0:T(8,128)(2,1)S(1)} %get-tuple-element.39), channel_id=1, source_target_pairs={{0,6},{1,7},{2,4},{3,5},{4,2},{5,3},{6,0},{7,1},{8,14},{9,15},{10,... | collective-permute-start | bytes 202760 | tf_op jit(solution)/shard_map/ppermute | solution.py:603
  42.8 1.7 %collective-permute-done.7.refs_4_ = bf16[264,128]{1,0:T(8,128)(2,1)S(1)} collective-permute-done((bf16[264,128]{1,0:T(8,128)(2,1)S(1)}, bf16[264,128]{1,0:T(8,128)(2,1)S(1)}, u32[]{:S(2)}, u32[]{:S(2)}) %collective-permute-start.7) | collective-permute-done | bytes 67616 | tf_op jit(solution)/shard_map/ppermute | solution.py:603
  44.5 4.3 %collective-permute-done.8.refs_5_ = bf16[264,128]{1,0:T(8,128)(2,1)S(1)} collective-permute-done((bf16[264,128]{1,0:T(8,128)(2,1)S(1)}, bf16[264,128]{1,0:T(8,128)(2,1)S(1)}, u32[]{:S(2)}, u32[]{:S(2)}) %collective-permute-start.8) | collective-permute-done | bytes 67616 | tf_op jit(solution)/shard_map/ppermute | solution.py:603
  48.8 1.6 %collective-permute-done.9.refs_6_ = bf16[264,128]{1,0:T(8,128)(2,1)S(1)} collective-permute-done((bf16[264,128]{1,0:T(8,128)(2,1)S(1)}, bf16[264,128]{1,0:T(8,128)(2,1)S(1)}, u32[]{:S(2)}, u32[]{:S(2)}) %collective-permute-start.9) | collective-permute-done | bytes 67616 | tf_op jit(solution)/shard_map/ppermute | solution.py:603
  50.4 3.0 %collective-permute-done.10.refs_7_ = bf16[264,128]{1,0:T(8,128)(2,1)S(1)} collective-permute-done((bf16[264,128]{1,0:T(8,128)(2,1)S(1)}, bf16[264,128]{1,0:T(8,128)(2,1)S(1)}, u32[]{:S(2)}, u32[]{:S(2)}) %collective-permute-start.10) | collective-permute-done | bytes 67616 | tf_op jit(solution)/shard_map/ppermute | solution.py:603
  53.4 1.3 %shard_map.105 = (bf16[2048,256]{1,0:T(8,128)(2,1)S(1)}, bf16[64,256]{1,0:T(8,128)(2,1)S(1)}, bf16[64,256]{1,0:T(8,128)(2,1)S(1)}, bf16[4,64,256]{2,1,0:T(8,128)(2,1)S(1)}) custom-call(s32[4,8]{1,0:T(4,128)S(1)} %pad_add_fusion.links, bf16[264,128]{1,0:T(8,128)(2,1)S(1)} %get-tuple-element.33.refs_0_, bf16[264,128]{1,0:T(8,128)(2,1)S(1)} %collective-permute-done.4.refs_1_, ...), custom_call_target="tpu_custom_call" | custom-call | tf_op jit(solution)/shard_map/pallas_call | solution.py:525
  55.6 1.9 %collective-permute-start.12 = (bf16[64,256]{1,0:T(8,128)(2,1)S(1)}, bf16[64,256]{1,0:T(8,128)(2,1)S(1)}, u32[]{:S(2)}, u32[]{:S(2)}) collective-permute-start(bf16[64,256]{1,0:T(8,128)(2,1)S(1)} %get-tuple-element.42), channel_id=1, source_target_pairs={{8,16},{16,8},{9,17},{17,9},{10,18},{18,10},{11,19},{19,11},{12,20... | collective-permute-start | bytes 98312 | tf_op jit(solution)/shard_map/ppermute | solution.py:33
  57.5 2.5 %shard_map.106.inner = bf16[1984,256]{1,0:T(8,128)(2,1)S(1)} custom-call(bf16[2048,256]{1,0:T(8,128)(2,1)S(1)} %get-tuple-element.43.bev, bf16[9,256,256]{2,1,0:T(8,128)(2,1)S(1)} %bitcast.18), custom_call_target="tpu_custom_call" | custom-call | tf_op jit(solution)/shard_map/pallas_call | solution.py:525
  61.5 2.6 %collective-permute-start.14 = (bf16[2,68,256]{2,1,0:T(8,128)(2,1)S(1)}, bf16[2,68,256]{2,1,0:T(8,128)(2,1)S(1)}, u32[]{:S(2)}, u32[]{:S(2)}) collective-permute-start(bf16[2,68,256]{2,1,0:T(8,128)(2,1)S(1)} %get-tuple-element.51), channel_id=1, source_target_pairs={{1,2},{2,1},{3,4},{4,3},{5,6},{6,5},{9,10},{10,9},{11,12},{12,11},... | collective-permute-start | bytes 208904 | tf_op jit(solution)/shard_map/ppermute | solution.py:33
  64.2 3.8 %second_core.1 = (bf16[64,32,256]{2,1,0:T(8,128)(2,1)}, f32[2,1024,128]{2,1,0:T(8,128)S(1)}, bf16[4,32,256]{2,1,0:T(8,128)(2,1)S(1)}) custom-call(s32[4,8]{1,0:T(4,128)S(1)} %pad_add_fusion.links, bf16[1984,256]{1,0:T(8,128)(2,1)S(1)} %shard_map.106.inner, bf16[2048,256]{1,0:T(8,128)(2,1)S(1)} %get-tuple-element.43.bev, ...), custom_call_target="tpu_custom_call" | custom-call | tf_op jit(solution)/shard_map/second_core/pallas_call | solution.py:648
  68.0 2.5 %edges.1 = bf16[64,32,256]{2,1,0:T(8,128)(2,1)} custom-call(s32[4,8]{1,0:T(4,128)S(1)} %pad_add_fusion.links, bf16[64,32,256]{2,1,0:T(8,128)(2,1)} %get-tuple-element.47.unused, f32[2,1024,128]{2,1,0:T(8,128)S(1)} %get-tuple-element.48.flanks, bf16[4,32,256]{2,1,0:T(8,128)(2,1)S(1)} %get-tuple-element.49.ends, ...), custom_call_target="tpu_custom_call", output_to_operand_aliasing={{}: (1, {})} | custom-call | tf_op jit(solution)/shard_map/edges/pallas_call | solution.py:666
  (44 shorter events, 7.6 us)
Async XLA Ops:
  0.7 1.2 %copy-start.1 = (bf16[8,512,128]{2,1,0:T(8,128)(2,1)S(1)}, bf16[8,512,128]{2,1,0:T(8,128)(2,1)}, u32[]{:S(2)}) copy-start(bf16[8,512,128]{2,1,0:T(8,128)(2,1)} %param.10) | copy-start | bytes 3145732
  2.9 13.6 %collective-permute-start = (bf16[1088,128]{1,0:T(8,128)(2,1)S(1)}, bf16[1088,128]{1,0:T(8,128)(2,1)S(1)}, u32[]{:S(2)}, u32[]{:S(2)}) collective-permute-start(bf16[1088,128]{1,0:T(8,128)(2,1)S(1)} %get-tuple-element.28), channel_id=1, source_target_pairs={{0,1},{1,0},{2,3},{3,2},{4,5},{5,4},{6,7},{7,6},{8,9},{9,8},{10,11... | collective-permute-start | bytes 835592 | tf_op jit(solution)/shard_map/ppermute | solution.py:32
  4.2 12.3 %collective-permute-start.1 = (bf16[1088,128]{1,0:T(8,128)(2,1)S(1)}, bf16[1088,128]{1,0:T(8,128)(2,1)S(1)}, u32[]{:S(2)}, u32[]{:S(2)}) collective-permute-start(bf16[1088,128]{1,0:T(8,128)(2,1)S(1)} %get-tuple-element.29), channel_id=1, source_target_pairs={{1,2},{2,1},{3,4},{4,3},{5,6},{6,5},{7,8},{8,7},{9,10},{10,9},{11,... | collective-permute-start | bytes 835592 | tf_op jit(solution)/shard_map/ppermute | solution.py:33
  10.8 10.4 %copy-start.2 = (bf16[8,512,128]{2,1,0:T(8,128)(2,1)S(1)}, bf16[8,512,128]{2,1,0:T(8,128)(2,1)}, u32[]{:S(2)}) copy-start(bf16[8,512,128]{2,1,0:T(8,128)(2,1)} %param.10) | copy-start | bytes 3145732
  10.8 10.4 %copy-start.6 = (bf16[7,128,128]{2,1,0:T(8,128)(2,1)S(1)}, bf16[7,128,128]{2,1,0:T(8,128)(2,1)}, u32[]{:S(2)}) copy-start(bf16[7,128,128]{2,1,0:T(8,128)(2,1)} %param.16) | copy-start | bytes 688132
  17.9 11.7 %collective-permute-start.2 = (bf16[1088,128]{1,0:T(8,128)(2,1)S(1)}, bf16[1088,128]{1,0:T(8,128)(2,1)S(1)}, u32[]{:S(2)}, u32[]{:S(2)}) collective-permute-start(bf16[1088,128]{1,0:T(8,128)(2,1)S(1)} %get-tuple-element.31), channel_id=1, source_target_pairs={{0,1},{1,0},{2,3},{3,2},{4,5},{5,4},{6,7},{7,6},{8,9},{9,8},{10,11... | collective-permute-start | bytes 835592 | tf_op jit(solution)/shard_map/ppermute | solution.py:32
  19.2 10.5 %collective-permute-start.3 = (bf16[1088,128]{1,0:T(8,128)(2,1)S(1)}, bf16[1088,128]{1,0:T(8,128)(2,1)S(1)}, u32[]{:S(2)}, u32[]{:S(2)}) collective-permute-start(bf16[1088,128]{1,0:T(8,128)(2,1)S(1)} %get-tuple-element.32), channel_id=1, source_target_pairs={{1,2},{2,1},{3,4},{4,3},{5,6},{6,5},{7,8},{8,7},{9,10},{10,9},{11,... | collective-permute-start | bytes 835592 | tf_op jit(solution)/shard_map/ppermute | solution.py:33
  21.3 8.4 %copy-start.4 = (bf16[4,1024,256]{2,1,0:T(8,128)(2,1)S(1)}, bf16[4,1024,256]{2,1,0:T(8,128)(2,1)}, u32[]{:S(2)}) copy-start(bf16[4,1024,256]{2,1,0:T(8,128)(2,1)} %height.1) | copy-start | bytes 6291460
  21.3 8.4 %copy-start.7 = (s32[8]{0:T(128)S(1)}, s32[8]{0:T(128)}, u32[]{:S(2)}) copy-start(s32[8]{0:T(128)} %param.12) | copy-start | bytes 100
  21.3 8.4 %copy-start.8 = (s32[8]{0:T(128)S(1)}, s32[8]{0:T(128)}, u32[]{:S(2)}) copy-start(s32[8]{0:T(128)} %param.13) | copy-start | bytes 100
  21.3 8.4 %copy-start.9 = (s32[1,16]{1,0:T(1,128)S(1)}, s32[1,16]{1,0:T(1,128)}, u32[]{:S(2)}) copy-start(s32[1,16]{1,0:T(1,128)} %columns.1) | copy-start | bytes 196
  29.7 27.9 %copy-start = (bf16[3,3,256,256]{3,2,1,0:T(8,128)(2,1)S(1)}, bf16[3,3,256,256]{3,2,1,0:T(8,128)(2,1)}, u32[]{:S(2)}) copy-start(bf16[3,3,256,256]{3,2,1,0:T(8,128)(2,1)} %param.18) | copy-start | bytes 3538948
  32.0 9.3 %collective-permute-start.4 = (bf16[264,128]{1,0:T(8,128)(2,1)S(1)}, bf16[264,128]{1,0:T(8,128)(2,1)S(1)}, u32[]{:S(2)}, u32[]{:S(2)}) collective-permute-start(bf16[264,128]{1,0:T(8,128)(2,1)S(1)} %get-tuple-element.34), channel_id=1, source_target_pairs={{0,1},{1,0},{2,3},{3,2},{4,5},{5,4},{6,7},{7,6},{8,9},{9,8},{10,11... | collective-permute-start | bytes 202760 | tf_op jit(solution)/shard_map/ppermute | solution.py:603
  34.3 8.2 %collective-permute-start.5 = (bf16[264,128]{1,0:T(8,128)(2,1)S(1)}, bf16[264,128]{1,0:T(8,128)(2,1)S(1)}, u32[]{:S(2)}, u32[]{:S(2)}) collective-permute-start(bf16[264,128]{1,0:T(8,128)(2,1)S(1)} %get-tuple-element.35), channel_id=1, source_target_pairs={{0,2},{1,3},{2,0},{3,1},{4,6},{5,7},{6,4},{7,5},{8,10},{9,11},{10,... | collective-permute-start | bytes 202760 | tf_op jit(solution)/shard_map/ppermute | solution.py:603
  34.5 8.3 %collective-permute-start.6 = (bf16[264,128]{1,0:T(8,128)(2,1)S(1)}, bf16[264,128]{1,0:T(8,128)(2,1)S(1)}, u32[]{:S(2)}, u32[]{:S(2)}) collective-permute-start(bf16[264,128]{1,0:T(8,128)(2,1)S(1)} %get-tuple-element.36), channel_id=1, source_target_pairs={{0,3},{1,2},{2,1},{3,0},{4,7},{5,6},{6,5},{7,4},{8,11},{9,10},{10,... | collective-permute-start | bytes 202760 | tf_op jit(solution)/shard_map/ppermute | solution.py:603
  35.6 8.9 %collective-permute-start.7 = (bf16[264,128]{1,0:T(8,128)(2,1)S(1)}, bf16[264,128]{1,0:T(8,128)(2,1)S(1)}, u32[]{:S(2)}, u32[]{:S(2)}) collective-permute-start(bf16[264,128]{1,0:T(8,128)(2,1)S(1)} %get-tuple-element.37), channel_id=1, source_target_pairs={{0,4},{1,5},{2,6},{3,7},{4,0},{5,1},{6,2},{7,3},{8,12},{9,13},{10,... | collective-permute-start | bytes 202760 | tf_op jit(solution)/shard_map/ppermute | solution.py:603
  40.2 8.6 %collective-permute-start.8 = (bf16[264,128]{1,0:T(8,128)(2,1)S(1)}, bf16[264,128]{1,0:T(8,128)(2,1)S(1)}, u32[]{:S(2)}, u32[]{:S(2)}) collective-permute-start(bf16[264,128]{1,0:T(8,128)(2,1)S(1)} %get-tuple-element.38), channel_id=1, source_target_pairs={{0,5},{1,4},{2,7},{3,6},{4,1},{5,0},{6,3},{7,2},{8,13},{9,12},{10,... | collective-permute-start | bytes 202760 | tf_op jit(solution)/shard_map/ppermute | solution.py:603
  41.3 9.1 %collective-permute-start.9 = (bf16[264,128]{1,0:T(8,128)(2,1)S(1)}, bf16[264,128]{1,0:T(8,128)(2,1)S(1)}, u32[]{:S(2)}, u32[]{:S(2)}) collective-permute-start(bf16[264,128]{1,0:T(8,128)(2,1)S(1)} %get-tuple-element.39), channel_id=1, source_target_pairs={{0,6},{1,7},{2,4},{3,5},{4,2},{5,3},{6,0},{7,1},{8,14},{9,15},{10,... | collective-permute-start | bytes 202760 | tf_op jit(solution)/shard_map/ppermute | solution.py:603
  42.5 10.9 %collective-permute-start.10 = (bf16[264,128]{1,0:T(8,128)(2,1)S(1)}, bf16[264,128]{1,0:T(8,128)(2,1)S(1)}, u32[]{:S(2)}, u32[]{:S(2)}) collective-permute-start(bf16[264,128]{1,0:T(8,128)(2,1)S(1)} %get-tuple-element.40), channel_id=1, source_target_pairs={{0,7},{1,6},{2,5},{3,4},{4,3},{5,2},{6,1},{7,0},{8,15},{9,14},{10,... | collective-permute-start | bytes 202760 | tf_op jit(solution)/shard_map/ppermute | solution.py:603
  54.7 9.4 %copy-start.3 = (bf16[3,3,256,256]{3,2,1,0:T(8,128)(2,1)S(1)}, bf16[3,3,256,256]{3,2,1,0:T(8,128)(2,1)}, u32[]{:S(2)}) copy-start(bf16[3,3,256,256]{3,2,1,0:T(8,128)(2,1)} %param.19) | copy-start | bytes 3538948
  54.7 5.4 %collective-permute-start.11 = (bf16[64,256]{1,0:T(8,128)(2,1)S(1)}, bf16[64,256]{1,0:T(8,128)(2,1)S(1)}, u32[]{:S(2)}, u32[]{:S(2)}) collective-permute-start(bf16[64,256]{1,0:T(8,128)(2,1)S(1)} %get-tuple-element.41), channel_id=1, source_target_pairs={{0,8},{8,0},{16,24},{24,16},{1,9},{9,1},{17,25},{25,17},{2,10},{10... | collective-permute-start | bytes 98312 | tf_op jit(solution)/shard_map/ppermute | solution.py:32
  55.6 5.2 %collective-permute-start.12 = (bf16[64,256]{1,0:T(8,128)(2,1)S(1)}, bf16[64,256]{1,0:T(8,128)(2,1)S(1)}, u32[]{:S(2)}, u32[]{:S(2)}) collective-permute-start(bf16[64,256]{1,0:T(8,128)(2,1)S(1)} %get-tuple-element.42), channel_id=1, source_target_pairs={{8,16},{16,8},{9,17},{17,9},{10,18},{18,10},{11,19},{19,11},{12,20... | collective-permute-start | bytes 98312 | tf_op jit(solution)/shard_map/ppermute | solution.py:33
  60.9 7.1 %collective-permute-start.13 = (bf16[2,68,256]{2,1,0:T(8,128)(2,1)S(1)}, bf16[2,68,256]{2,1,0:T(8,128)(2,1)S(1)}, u32[]{:S(2)}, u32[]{:S(2)}) collective-permute-start(bf16[2,68,256]{2,1,0:T(8,128)(2,1)S(1)} %get-tuple-element.52), channel_id=1, source_target_pairs={{0,1},{1,0},{2,3},{3,2},{4,5},{5,4},{6,7},{7,6},{8,9},{9,8},{10,11... | collective-permute-start | bytes 208904 | tf_op jit(solution)/shard_map/ppermute | solution.py:32
  61.5 6.5 %collective-permute-start.14 = (bf16[2,68,256]{2,1,0:T(8,128)(2,1)S(1)}, bf16[2,68,256]{2,1,0:T(8,128)(2,1)S(1)}, u32[]{:S(2)}, u32[]{:S(2)}) collective-permute-start(bf16[2,68,256]{2,1,0:T(8,128)(2,1)S(1)} %get-tuple-element.51), channel_id=1, source_target_pairs={{1,2},{2,1},{3,4},{4,3},{5,6},{6,5},{9,10},{10,9},{11,12},{12,11},... | collective-permute-start | bytes 208904 | tf_op jit(solution)/shard_map/ppermute | solution.py:33
  (1 other events, 0.9 us)
